TPU v7x, 512 devices: a whole 4x8x8 slice. The times are simulated.
512 devices in a mesh: ctx: 64 (over z, y), mod: 8 (over x, core).
Axes of the slice: x: 4, y: 8, z: 8, core: 2. Of those that a mesh axis runs over, the one named last changes fastest.
Arguments:
- seq_input: float32 [8192, 4096], P('ctx', 'mod'), may hold values from -6 to 6
- log_decay: float32 [64, 8192], P('mod', 'ctx'), may hold values from -0.7 to 0
- b_proj: float32 [8192, 128], P('ctx'), may hold values from -0.2 to 0.2
- c_proj: float32 [8192, 128], P('ctx'), may hold values from -0.2 to 0.2
- skip_gain: float32 [64], P('mod'), may hold values from 0.1 to 1.9
- down_weight: float32 [2, 4096, 256], P(None, 'mod'), may hold values from -0.09375 to 0.09375
- up_weight: float32 [2, 256, 4096], P(None, None, 'mod'), may hold values from -0.375 to 0.375
- block_lang: int32 [64], P('ctx'), may hold values from 0 to 1
- cotangent: float32 [8192, 4096], P('ctx', 'mod'), may hold values from -6 to 6
Outputs:
- layer_out: float32 [8192, 4096], P('ctx', 'mod')
- input_grad: float32 [8192, 4096], P('ctx', 'mod')
- b_grad: float32 [8192, 128], P('ctx')
- c_grad: float32 [8192, 128], P('ctx')
- down_grad: float32 [2, 4096, 256], P(None, 'mod', 'ctx')
- up_grad: float32 [2, 256, 4096], P(None, 'ctx', 'mod')
All inputs are finite; a program needn't handle non-finite values.
Results may differ from a plain program's by a relative error of at most 0.0003.
Values sent between devices are 32-bit elements; how exact they have to be, the bound alone decides.
A program may use at most 128 MiB of HBM per device.

v0:
```python
import jax
import jax.numpy as jnp
from jax import lax
from jax.sharding import PartitionSpec as P

P_SIZE = 64
R = 256
LANG = 2
BLK = 128


highest = lax.Precision.HIGHEST


def carried_in(part, axis, combine, identity, reverse):
    count = lax.axis_size(axis)
    place = lax.axis_index(axis)
    ahead = count - 1 - place if reverse else place
    gathered = jax.tree.map(lambda a: lax.all_gather(a, axis), part)
    state = jax.tree.map(lambda a, e: jnp.zeros_like(a) + jnp.asarray(e, a.dtype), part, identity)

    def one(step, state):
        source = count - 1 - step if reverse else step
        return combine(
            state, jax.tree.map(lambda a: lax.dynamic_index_in_dim(a, source, 0, False), gathered)
        )

    return lax.fori_loop(0, ahead, one, state)


def merge_states(earlier, following):
    return (earlier[0] * following[0], following[0][:, None, None] * earlier[1] + following[1])


def silu_slope(values):
    sigmoid_v = jax.nn.sigmoid(values)
    return sigmoid_v * (1.0 + values * (1.0 - sigmoid_v))


def shards(
    seq_input, log_decay, b_proj, c_proj, skip_gain, down_weight, up_weight, block_lang, cotangent
):
    row_count = seq_input.shape[0]
    head_count = log_decay.shape[0]
    width = seq_input.shape[1]
    heads_in = seq_input.reshape(row_count, head_count, P_SIZE)
    cumulative = jnp.cumsum(log_decay, axis=1)
    lower_mask = jnp.tril(jnp.ones((row_count, row_count), bool))
    gaps = cumulative[:, :, None] - cumulative[:, None, :]
    decay_mask = jnp.where(lower_mask, jnp.exp(jnp.where(lower_mask, gaps, 0.0)), 0.0)
    scores = jnp.dot(c_proj, b_proj.T, precision=highest)
    mixing = decay_mask * scores
    tail_decay = jnp.exp(cumulative[:, -1:] - cumulative)
    total_decay = jnp.exp(cumulative[:, -1])
    head_decay = jnp.exp(cumulative)
    local_state = jnp.einsum("hs,shp,sn->hpn", tail_decay, heads_in, b_proj, precision=highest)
    unit_decay = jnp.ones_like(total_decay)
    empty_state = jnp.zeros_like(local_state)
    carried = carried_in(
        (total_decay, local_state), "ctx", merge_states, (unit_decay, empty_state), False
    )
    state_in = carried[1]
    hidden_heads = jnp.einsum("hts,shp->thp", mixing, heads_in, precision=highest)
    hidden_heads = hidden_heads + head_decay.T[:, :, None] * jnp.einsum(
        "hpn,tn->thp", state_in, c_proj, precision=highest
    )
    hidden_heads = hidden_heads + skip_gain[None, :, None] * heads_in
    hidden = hidden_heads.reshape(row_count, width)
    lang_tok = jnp.repeat(block_lang, BLK)
    one_hot = (lang_tok[:, None] == jnp.arange(LANG, dtype=jnp.int32)[None, :]).astype(jnp.float32)
    flat_down = down_weight.transpose(1, 0, 2).reshape(width, LANG * R)
    flat_up = up_weight.reshape(LANG * R, width)
    pre_all = jnp.dot(hidden, flat_down, precision=highest).reshape(row_count, LANG, R)
    pre_part = jnp.einsum("tk,tkr->tr", one_hot, pre_all, precision=highest)
    pre_act = lax.psum(pre_part, "mod")
    active = jax.nn.silu(pre_act)
    spread = (one_hot[:, :, None] * active[:, None, :]).reshape(row_count, LANG * R)
    layer_out = hidden + jnp.dot(spread, flat_up, precision=highest)
    back_all = jnp.dot(cotangent, flat_up.T, precision=highest).reshape(row_count, LANG, R)
    back_part = jnp.einsum("tk,tkr->tr", one_hot, back_all, precision=highest)
    back_act = lax.psum(back_part, "mod")
    pre_grad = back_act * silu_slope(pre_act)
    spread_grad = (one_hot[:, :, None] * pre_grad[:, None, :]).reshape(row_count, LANG * R)
    hidden_grad = cotangent + jnp.dot(spread_grad, flat_down.T, precision=highest)
    down_term = (
        jnp.dot(hidden.T, spread_grad, precision=highest).reshape(width, LANG, R).transpose(1, 0, 2)
    )
    up_term = jnp.dot(spread.T, cotangent, precision=highest).reshape(LANG, R, width)
    down_grad, up_grad = (
        lax.psum_scatter(down_term, "ctx", scatter_dimension=2, tiled=True),
        lax.psum_scatter(up_term, "ctx", scatter_dimension=1, tiled=True),
    )
    grad_heads = hidden_grad.reshape(row_count, head_count, P_SIZE)
    local_adjoint = jnp.einsum("hs,shp,sn->hpn", head_decay, grad_heads, c_proj, precision=highest)
    incoming = carried_in(
        (total_decay, local_adjoint), "ctx", merge_states, (unit_decay, empty_state), True
    )
    adjoint_in = incoming[1]
    input_heads = jnp.einsum("hts,thp->shp", mixing, grad_heads, precision=highest)
    input_heads = input_heads + tail_decay.T[:, :, None] * jnp.einsum(
        "hpn,sn->shp", adjoint_in, b_proj, precision=highest
    )
    input_heads = input_heads + skip_gain[None, :, None] * grad_heads
    input_grad = input_heads.reshape(row_count, width)
    weighted = decay_mask * jnp.einsum("thp,shp->hts", grad_heads, heads_in, precision=highest)
    b_part = jnp.einsum("hts,tn->sn", weighted, c_proj, precision=highest)
    b_part = b_part + jnp.einsum(
        "hs,shp,hpn->sn", tail_decay, heads_in, adjoint_in, precision=highest
    )
    c_part = jnp.einsum("hts,sn->tn", weighted, b_proj, precision=highest)
    c_part = c_part + jnp.einsum(
        "ht,thp,hpn->tn", head_decay, grad_heads, state_in, precision=highest
    )
    b_grad, c_grad = lax.psum((b_part, c_part), "mod")
    return (layer_out, input_grad, b_grad, c_grad, down_grad, up_grad)


def solution(mesh):
    return jax.shard_map(
        shards,
        mesh=mesh,
        in_specs=(
            P("ctx", "mod"),
            P("mod", "ctx"),
            P("ctx", None),
            P("ctx", None),
            P("mod"),
            P(None, "mod", None),
            P(None, None, "mod"),
            P("ctx"),
            P("ctx", "mod"),
        ),
        out_specs=(
            P("ctx", "mod"),
            P("ctx", "mod"),
            P("ctx", None),
            P("ctx", None),
            P(None, "mod", "ctx"),
            P(None, "ctx", "mod"),
        ),
        check_vma=False,
    )
```

profile of v0, /device:TPU:1, one launch (start us, length us, event | category | flops | bytes accessed | tf_op | source)
XLA Modules:
  0.0 854.2 jit_solution(9183198847145956088)
XLA Ops:
  7.2 1.1 reduce_window_sum.11
  8.6 1.1 copy.29
  9.7 2.0 fusion.39
  11.7 1.4 fusion.59
  14.1 127.9 %all-reduce = f32[512]{0:T(512)S(1)} all-reduce(f32[512]{0:T(512)S(1)} %dynamic-update-slice), channel_id=2, replica_groups=mesh['ctx'=64,'mod'=8] {'ctx'}, use_global_device_ids=true, to_apply=%add | all-reduce | flops 512 | bytes 4096
  142.6 1.6 copy.30
  144.9 2.1 fusion.17
  148.5 1.1 fusion.60
  149.7 8.9 %all-gather.6.cloned.1.call-done = f32[512,64,128]{2,1,0:T(8,128)} async-done(((f32[8,64,128]{2,1,0:T(8,128)}), f32[512,64,128]{2,1,0:T(8,128)}) %all-gather.6.cloned.1.call-update) | async-done | bytes 16777232 | tf_op jit(solution)/shard_map/all_gather | solution.py:19
  158.6 1.2 fusion.4
  159.8 2.3 fusion.5
  162.1 1.3 fusion.9
  163.4 1.4 fusion.31
  165.7 190.0 %all-reduce.14.cloned.1.call-done = (f32[128,256]{0,1:T(8,128)}, f32[128,256]{0,1:T(8,128)}) async-done(((f32[128,256]{0,1:T(8,128)}, f32[128,256]{0,1:T(8,128)}), (f32[128,256]{0,1:T(8,128)}, f32[128,256]{0,1:T(8,128)})) %all-reduce.14.cloned.1.call-update) | async-done | bytes 262160 | tf_op jit(solution)/shard_map/psum | solution.py:75
  357.5 1.9 convolution_bitcast_fusion
  359.5 1.3 copy.37
  360.8 3.0 fusion.15
  363.9 2.3 fusion.8
  366.4 1.9 fusion.36
  369.2 1.1 copy.33
  370.9 2.0 fusion
  372.9 1.7 convolution_add_fusion
  374.6 1.5 fusion.7
  376.1 148.6 %all-reduce.10.cloned.1.call-done = (f32[2,512,256]{1,0,2:T(2,128)}, f32[2,256,512]{2,1,0:T(8,128)}) async-done(((f32[2,512,256]{1,0,2:T(2,128)}, f32[2,256,512]{2,1,0:T(8,128)}), (f32[2,512,256]{1,0,2:T(2,128)}, f32[2,256,512]{2,1,0:T(8,128)})) %all-reduce.10.cloned.1.call-update) | async-done | bytes 2097168
  526.0 1.4 constant_dynamic-slice_fusion
  527.4 140.1 %all-gather.8.cloned.1.call-done = f32[512,64,128]{2,1,0:T(8,128)} async-done(((f32[8,64,128]{2,1,0:T(8,128)}), f32[512,64,128]{2,1,0:T(8,128)}) %all-gather.8.cloned.1.call-update) | async-done | bytes 16777232 | tf_op jit(solution)/shard_map/all_gather | solution.py:19
  667.5 112.1 %while.27 = (s32[]{:T(128)}, f32[8,64,128]{2,1,0:T(8,128)S(1)}, s32[]{:T(128)}, f32[64,8]{1,0:T(8,128)}, f32[64,8,64,128]{3,2,1,0:T(8,128)}, /*index=5*/s32[]{:T(128)}, s32[]{:T(128)}, s32[]{:T(128)}, s32[]{:T(128)}) while((s32[]{:T(128)}, f32[8,64,128]{2,1,0:T(8,128)S(1)}, s32[]{:T(128)}, f32[64,8]{1,0:T(8,128)}, ...), condition=%wide.region_6.7_spmd, body=%wide.region_5.6_spmd.sunk | while | flops 131078 | bytes 786675 | solution.py:28
  668.2 1.1 bitcast_add_fusion.5
  670.0 1.1 bitcast_add_fusion.5
  671.8 1.1 bitcast_add_fusion.5
  673.6 1.1 bitcast_add_fusion.5
  675.4 1.1 bitcast_add_fusion.5
  677.1 1.1 bitcast_add_fusion.5
  678.9 1.1 bitcast_add_fusion.5
  680.7 1.1 bitcast_add_fusion.5
  682.5 1.1 bitcast_add_fusion.5
  684.3 1.1 bitcast_add_fusion.5
  686.0 1.1 bitcast_add_fusion.5
  687.8 1.1 bitcast_add_fusion.5
  689.6 1.1 bitcast_add_fusion.5
  691.4 1.1 bitcast_add_fusion.5
  693.2 1.1 bitcast_add_fusion.5
  694.9 1.1 bitcast_add_fusion.5
  696.7 1.1 bitcast_add_fusion.5
  698.5 1.1 bitcast_add_fusion.5
  700.3 1.1 bitcast_add_fusion.5
  702.1 1.1 bitcast_add_fusion.5
  703.8 1.1 bitcast_add_fusion.5
  705.6 1.1 bitcast_add_fusion.5
  707.4 1.1 bitcast_add_fusion.5
  709.2 1.1 bitcast_add_fusion.5
  711.0 1.1 bitcast_add_fusion.5
  712.7 1.1 bitcast_add_fusion.5
  714.5 1.1 bitcast_add_fusion.5
  716.3 1.1 bitcast_add_fusion.5
  718.1 1.1 bitcast_add_fusion.5
  719.9 1.1 bitcast_add_fusion.5
  779.7 1.5 convolution_bitcast_fusion.8
  781.2 1.2 fusion.3
  782.4 1.8 convolution_add_fusion.1
  784.2 1.4 fusion.6
  786.5 58.2 %all-reduce.12.cloned.1.call-done = (f32[128,128]{1,0:T(8,128)}, f32[128,128]{1,0:T(8,128)}) async-done(((f32[128,128]{1,0:T(8,128)}, f32[128,128]{1,0:T(8,128)}), (f32[128,128]{1,0:T(8,128)}, f32[128,128]{1,0:T(8,128)})) %all-reduce.12.cloned.1.call-update) | async-done | bytes 131088 | tf_op jit(solution)/shard_map/psum | solution.py:114
  844.7 1.5 copy.81
  846.2 1.5 copy.82
  (148 shorter events, 87.5 us)
Async XLA Ops:
  7.2 137.7 %copy-start = (f32[2,256,512]{2,1,0:T(8,128)S(1)}, f32[2,256,512]{2,1,0:T(8,128)}, u32[]{:S(2)}) copy-start(f32[2,256,512]{2,1,0:T(8,128)} %param.19) | copy-start | bytes 3145732
  7.2 356.7 %copy-start.1 = (f32[2,512,256]{2,1,0:T(8,128)S(1)}, f32[2,512,256]{2,1,0:T(8,128)}, u32[]{:S(2)}) copy-start(f32[2,512,256]{2,1,0:T(8,128)} %param.18) | copy-start | bytes 3145732
  7.2 151.3 %all-gather.6.cloned.1.call-start = ((), (), s32[]{:S(2)}) async-start(), calls=%async_computation | async-start | bytes 17039360 | tf_op jit(solution)/shard_map/all_gather | solution.py:19
  9.7 148.8 %copy-start.2 = (f32[128,512]{0,1:T(8,128)}, f32[128,512]{0,1:T(8,128)S(1)}, u32[]{:S(2)}) copy-start(f32[128,512]{0,1:T(8,128)S(1)} %copy.29) | copy-start | bytes 786436
  11.7 343.9 %all-reduce.14.cloned.1.call-start = ((), (), s32[]{:S(2)}) async-start(), calls=%async_computation.4 | async-start | bytes 524288 | tf_op jit(solution)/shard_map/psum | solution.py:75
  144.9 2.2 copy-start.9
  148.5 209.0 %copy-start.7 = (pred[128,128]{1,0:T(8,128)(4,1)}, pred[128,128]{1,0:T(8,128)(4,1)S(1)}, u32[]{:S(2)}) copy-start(pred[128,128]{1,0:T(8,128)(4,1)S(1)} %iota_compare_fusion) | copy-start | bytes 49156
  149.7 207.9 %copy-start.5 = (f32[128,128]{1,0:T(8,128)}, f32[128,128]{1,0:T(8,128)S(1)}, u32[]{:S(2)}) copy-start(f32[128,128]{1,0:T(8,128)S(1)} %fusion.60) | copy-start | bytes 196612
  162.1 1.3 copy-start.3
  165.5 359.1 %all-reduce.10.cloned.1.call-start = ((), (), s32[]{:S(2)}) async-start(), calls=%async_computation.2 | async-start | bytes 4194304
  356.7 0.9 copy-start.4
  360.8 423.4 %copy-start.6 = (f32[128,128]{1,0:T(8,128)S(1)}, f32[128,128]{1,0:T(8,128)}, u32[]{:S(2)}) copy-start(f32[128,128]{1,0:T(8,128)} %copy-done.5) | copy-start | bytes 196612
  360.8 423.5 %copy-start.8 = (pred[128,128]{1,0:T(8,128)(4,1)S(1)}, pred[128,128]{1,0:T(8,128)(4,1)}, u32[]{:S(2)}) copy-start(pred[128,128]{1,0:T(8,128)(4,1)} %copy-done.7) | copy-start | bytes 49156
  363.9 303.6 %all-gather.8.cloned.1.call-start = ((), (), s32[]{:S(2)}) async-start(), calls=%async_computation.1 | async-start | bytes 17039360 | tf_op jit(solution)/shard_map/all_gather | solution.py:19
  368.3 476.4 %all-reduce.12.cloned.1.call-start = ((), (), s32[]{:S(2)}) async-start(), calls=%async_computation.3 | async-start | bytes 262144 | tf_op jit(solution)/shard_map/psum | solution.py:114
Sparse Core Ops, SparseCore 0:
  11.8 146.6 all-gather.5
  165.7 189.9 all-reduce.13
  364.0 160.6 all-reduce.9
  527.6 139.8 all-gather.7
  784.3 60.3 all-reduce.11
where the time goes:
time: 860 us; the launch traced here: 854 us
  waiting for transfers between devices  546 us (63%)
  blocking collectives  128 us (15%)
  other arithmetic  69.5 us (8%)
  local copies, waits for them, and re-layouts  59.7 us (7%)
  matrix products  33 us (4%)
  between operations  16 us (2%)
    psum x1, waiting for transfers between devices, shards(): pre_act = lax.psum(pre_part, 'mod')  190 us
    all_gather x2, waiting for transfers between devices, carried_in(): gathered = jax.tree.map(lambda a: lax.all_gather(a, axis), part)  149 us
    unnamed x6, waiting for transfers between devices  149 us
    unnamed x1, blocking collectives  128 us
    add x63, other arithmetic, merge_states(): following[0][:, None, None] * earlier[1] + following[1]  66.4 us
    psum x1, waiting for transfers between devices, shards(): b_grad, c_grad = lax.psum((b_part, c_part), 'mod')  58.2 us
    mul x63, local copies, waits for them, and re-layouts, merge_states(): following[0][:, None, None] * earlier[1] + following[1]  43.9 us
  transfers between devices with their start and end apart: 5, of which 5 were waited for; matrix products, arithmetic and copies ran while one was open for 3% of the time, Pallas kernels for 0%

commit v1 on v0

v1 whole, which is shorter than its diff:
```python
import functools

import jax
import jax.numpy as jnp
from jax import lax
from jax.experimental import pallas as pl
from jax.experimental.pallas import tpu as pltpu
from jax.sharding import PartitionSpec as P

P_SIZE = 64
R = 256
LANG = 2
NY = 8
NZ = 8
NMOD = 8
f32 = jnp.float32
MESH = pl.DeviceIdType.MESH
high = lax.Precision.HIGH
VM = pl.BlockSpec(memory_space=pltpu.VMEM)
DMA = pltpu.SemaphoreType.DMA


def rcopy(src, dst, ss, rs, dev):
    return pltpu.make_async_remote_copy(
        src_ref=src, dst_ref=dst, send_sem=ss, recv_sem=rs, device_id=dev, device_id_type=MESH
    )


def ctx_place():
    c = lax.axis_index("ctx")
    return c // NY, c % NY


def y_dev(z, y, d):
    return {"ctx": z * NY + (y + d) % NY}


def z_dev(z, y, d):
    return {"ctx": ((z + d) % NZ) * NY + y}


def meet_ctx(z, y):
    barrier = pltpu.get_barrier_semaphore()
    for d in range(1, NY):
        pl.semaphore_signal(barrier, inc=1, device_id=y_dev(z, y, d), device_id_type=MESH)
    for d in range(1, NZ):
        pl.semaphore_signal(barrier, inc=1, device_id=z_dev(z, y, d), device_id_type=MESH)
    pl.semaphore_wait(barrier, NY + NZ - 2)


def scan_kernel(
    reverse, st_ref, aux_ref, out_ref, auxy_ref,
    gat, gaux, pre, pdec, tot, zg, ret, retin,
    s1, r1, s2, r2, s3, r3, s4, r4,
):
    z, y = ctx_place()
    meet_ctx(z, y)
    first = []
    for d in range(1, NY):
        peer = (y + d) % NY
        a = rcopy(aux_ref.at[peer], gaux.at[d], s2.at[d], r2.at[d], y_dev(z, y, d))
        b = rcopy(st_ref.at[peer], gat.at[d], s1.at[d], r1.at[d], y_dev(z, y, d))
        a.start()
        b.start()
        first += [a, b]
    gat[0] = st_ref[y]
    gaux[0] = aux_ref[y]
    for cp in first:
        cp.wait_recv()
    state = jnp.zeros((P_SIZE, 128), f32)
    dec = jnp.ones((1, 128), f32)
    order = range(NY - 1, -1, -1) if reverse else range(NY)
    for s in order:
        slot = (y - s + NY) % NY
        pre[s] = state
        pdec[s] = jnp.broadcast_to(dec, (8, 128))
        dd = gaux[slot][0:1]
        state = dd * state + gat[slot]
        dec = dd * dec
    tot[0:P_SIZE] = state
    tot[P_SIZE:] = jnp.broadcast_to(dec, (8, 128))
    second = []
    for d in range(1, NZ):
        cp = rcopy(tot, zg.at[d], s3.at[d], r3.at[d], z_dev(z, y, d))
        cp.start()
        second.append(cp)
    auxy_ref[...] = gaux[...]
    zg[0] = tot[...]
    for cp in second:
        cp.wait_recv()
    carry = jnp.zeros((P_SIZE, 128), f32)
    for s in (range(NZ - 1, -1, -1) if reverse else range(NZ)):
        blk = zg[(z - s + NZ) % NZ]
        nxt = blk[P_SIZE : P_SIZE + 1] * carry + blk[0:P_SIZE]
        use = (z < s) if reverse else (z > s)
        carry = jnp.where(use, nxt, carry)
    third = []
    for d in range(1, NY):
        s = (y + d) % NY
        ret[d] = pre[s] + pdec[s][0:1] * carry
        cp = rcopy(ret.at[d], retin.at[d], s4.at[d], r4.at[d], y_dev(z, y, d))
        cp.start()
        third.append(cp)
    retin[0] = pre[y] + pdec[y][0:1] * carry
    for cp in third:
        cp.wait_recv()
    for h in range(NY):
        out_ref[h] = retin[(y - h + NY) % NY]
    for cp in first + second + third:
        cp.wait_send()


def scan_call(state, aux, reverse, cid):
    return pl.pallas_call(
        functools.partial(scan_kernel, reverse),
        name="carry_rev" if reverse else "carry_fwd",
        out_shape=(
            jax.ShapeDtypeStruct((NY, P_SIZE, 128), f32),
            jax.ShapeDtypeStruct((NY, 8, 128), f32),
        ),
        in_specs=[VM, VM],
        out_specs=(VM, VM),
        scratch_shapes=[
            pltpu.VMEM((NY, P_SIZE, 128), f32),
            pltpu.VMEM((NY, 8, 128), f32),
            pltpu.VMEM((NY, P_SIZE, 128), f32),
            pltpu.VMEM((NY, 8, 128), f32),
            pltpu.VMEM((P_SIZE + 8, 128), f32),
            pltpu.VMEM((NZ, P_SIZE + 8, 128), f32),
            pltpu.VMEM((NY, P_SIZE, 128), f32),
            pltpu.VMEM((NY, P_SIZE, 128), f32),
        ]
        + [DMA((8,))] * 8,
        compiler_params=pltpu.CompilerParams(collective_id=cid, has_side_effects=True),
    )(state, aux)


def sum_kernel(x_ref, out_ref, buf, acc, ag, s1, r1, s2, r2):
    m = lax.axis_index("mod")
    barrier = pltpu.get_barrier_semaphore()
    for d in range(1, NMOD):
        pl.semaphore_signal(
            barrier, inc=1, device_id={"mod": (m + d) % NMOD}, device_id_type=MESH
        )
    pl.semaphore_wait(barrier, NMOD - 1)
    first, second = [], []
    for d in range(1, NMOD):
        peer = (m + d) % NMOD
        cp = rcopy(x_ref.at[peer], buf.at[d], s1.at[d], r1.at[d], {"mod": peer})
        cp.start()
        first.append(cp)
    total = x_ref[m]
    for d in range(1, NMOD):
        first[d - 1].wait_recv()
        total = total + buf[d]
    acc[...] = total
    for d in range(1, NMOD):
        cp = rcopy(acc, ag.at[d], s2.at[d], r2.at[d], {"mod": (m + d) % NMOD})
        cp.start()
        second.append(cp)
    ag[0] = total
    for cp in second:
        cp.wait_recv()
    for h in range(NMOD):
        out_ref[h] = ag[(m - h + NMOD) % NMOD]
    for cp in first + second:
        cp.wait_send()


def sum_call(x, cid):
    rows, cols = x.shape
    part = (NMOD, rows // NMOD, cols)
    out = pl.pallas_call(
        sum_kernel,
        name="sum_mod_%d" % cid,
        out_shape=jax.ShapeDtypeStruct(part, f32),
        in_specs=[VM],
        out_specs=VM,
        scratch_shapes=[pltpu.VMEM(part, f32), pltpu.VMEM(part[1:], f32), pltpu.VMEM(part, f32)]
        + [DMA((8,))] * 4,
        compiler_params=pltpu.CompilerParams(collective_id=cid, has_side_effects=True),
    )(x.reshape(part))
    return out.reshape(rows, cols)


def grad_kernel(g_ref, lang_ref, out_ref, buf, part, zbuf, s1, r1, s2, r2):
    z, y = ctx_place()
    meet_ctx(z, y)
    first, second = [], []
    for d in range(1, NY):
        cp = rcopy(g_ref.at[(y + d) % NY], buf.at[d], s1.at[d], r1.at[d], y_dev(z, y, d))
        cp.start()
        first.append(cp)
    buf[0] = g_ref[y]
    for cp in first:
        cp.wait_recv()

    @pl.loop(0, NZ)
    def _(t):
        zero = jnp.zeros((8, 512), f32)
        a, b = zero, zero
        for d in range(NY):
            v = buf[d, t]
            w = jnp.broadcast_to(lang_ref[d][1:2, 0:1], (8, 512))
            a = a + jnp.where(w < 0.5, v, 0.0)
            b = b + jnp.where(w < 0.5, 0.0, v)
        part[t, 0] = a
        part[t, 1] = b

    for d in range(1, NZ):
        cp = rcopy(part.at[(z + d) % NZ], zbuf.at[d], s2.at[d], r2.at[d], z_dev(z, y, d))
        cp.start()
        second.append(cp)
    total = part[z]
    for d in range(1, NZ):
        second[d - 1].wait_recv()
        total = total + zbuf[d]
    out_ref[...] = total
    for cp in first + second:
        cp.wait_send()


def grad_call(g, lang, cid):
    return pl.pallas_call(
        grad_kernel,
        name="weight_grads",
        out_shape=jax.ShapeDtypeStruct((LANG, 8, 512), f32),
        in_specs=[VM, VM],
        out_specs=VM,
        scratch_shapes=[
            pltpu.VMEM((NY, NZ, 8, 512), f32),
            pltpu.VMEM((NZ, LANG, 8, 512), f32),
            pltpu.VMEM((NZ, LANG, 8, 512), f32),
        ]
        + [DMA((8,))] * 4,
        compiler_params=pltpu.CompilerParams(collective_id=cid, has_side_effects=True),
    )(g, lang)


def ein(spec, *args):
    return jnp.einsum(spec, *args, precision=high)


def shards(
    seq_input, log_decay, b_proj, c_proj, skip_gain, down_weight, up_weight, block_lang, cotangent
):
    rows, width = seq_input.shape
    heads = log_decay.shape[0]
    x = seq_input.reshape(rows, heads, P_SIZE)
    cumulative = jnp.cumsum(log_decay, axis=1)
    lower = jnp.tril(jnp.ones((rows, rows), bool))
    gaps = cumulative[:, :, None] - cumulative[:, None, :]
    decay_mask = jnp.where(lower, jnp.exp(jnp.where(lower, gaps, 0.0)), 0.0)
    mixing = decay_mask * ein("tn,sn->ts", c_proj, b_proj)
    tail = jnp.exp(cumulative[:, -1:] - cumulative)
    total = jnp.exp(cumulative[:, -1])
    head = jnp.exp(cumulative)
    lang = block_lang[0]
    down = lax.dynamic_index_in_dim(down_weight, lang, 0, False)
    up = lax.dynamic_index_in_dim(up_weight, lang, 0, False)

    aux = jnp.where(
        jnp.arange(8)[None, :, None] == 0, total[:, None, None], lang.astype(f32)
    ) + jnp.zeros((heads, 8, 128), f32)
    local_state = ein("shp,sn->hpn", tail.T[:, :, None] * x, b_proj)
    state_in, aux_y = scan_call(local_state, aux, False, 1)
    hidden = ein("hts,shp->thp", mixing, x)
    hidden = hidden + skip_gain[None, :, None] * x
    hidden = hidden + head.T[:, :, None] * ein("hpn,tn->thp", state_in, c_proj)
    hidden = hidden.reshape(rows, width)
    pre_part = ein("tf,fr->tr", hidden, down)
    back_part = ein("tf,rf->tr", cotangent, up)
    both = sum_call(jnp.concatenate([pre_part, back_part], axis=1), 2)
    pre_act, back_act = both[:, :R], both[:, R:]
    gate = jax.nn.sigmoid(pre_act)
    active = pre_act * gate
    pre_grad = back_act * (gate * (1.0 + pre_act * (1.0 - gate)))
    hidden_grad = cotangent + ein("tr,fr->tf", pre_grad, down)
    gh = hidden_grad.reshape(rows, heads, P_SIZE)
    local_adjoint = ein("shp,sn->hpn", head.T[:, :, None] * gh, c_proj)
    adjoint_in, _ = scan_call(local_adjoint, aux, True, 3)

    layer_out = hidden + ein("tr,rf->tf", active, up)
    down_t = ein("tr,tf->rf", pre_grad, hidden).reshape(NZ, NY, 4, width)
    up_t = ein("tr,tf->rf", active, cotangent).reshape(NZ, NY, 4, width)
    g = jnp.concatenate([down_t, up_t], axis=2).transpose(1, 0, 2, 3)
    wg = grad_call(g, aux_y, 4)
    down_grad = wg[:, :4].transpose(0, 2, 1)
    up_grad = wg[:, 4:]

    input_grad = ein("hts,thp->shp", mixing, gh) + skip_gain[None, :, None] * gh
    input_grad = input_grad + tail.T[:, :, None] * ein("hpn,sn->shp", adjoint_in, b_proj)
    weighted = jnp.sum(decay_mask * ein("thp,shp->hts", gh, x), axis=0)
    b_part = ein("ts,tn->sn", weighted, c_proj)
    b_part = b_part + ein("shp,hpn->sn", tail.T[:, :, None] * x, adjoint_in)
    c_part = ein("ts,sn->tn", weighted, b_proj)
    c_part = c_part + ein("thp,hpn->tn", head.T[:, :, None] * gh, state_in)
    bc = sum_call(jnp.concatenate([b_part, c_part], axis=1), 5)
    return (layer_out, input_grad.reshape(rows, width), bc[:, :128], bc[:, 128:], down_grad, up_grad)


def solution(mesh):
    return jax.shard_map(
        shards,
        mesh=mesh,
        in_specs=(
            P("ctx", "mod"),
            P("mod", "ctx"),
            P("ctx", None),
            P("ctx", None),
            P("mod"),
            P(None, "mod", None),
            P(None, None, "mod"),
            P("ctx"),
            P("ctx", "mod"),
        ),
        out_specs=(
            P("ctx", "mod"),
            P("ctx", "mod"),
            P("ctx", None),
            P("ctx", None),
            P(None, "mod", "ctx"),
            P(None, "ctx", "mod"),
        ),
        check_vma=False,
    )
```

time: 860 us -> 166 us (0.19)
  waiting for transfers between devices: 546 us -> 0 us
  Pallas kernels: 0 us -> 141 us
  blocking collectives: 128 us -> 0 us
  other arithmetic: 69.5 us -> 3.13 us
  local copies, waits for them, and re-layouts: 59.7 us -> 7.97 us
  matrix products: 33 us -> 11.9 us
  between operations: 16 us -> 1.72 us
    psum x2 -> x0, waiting for transfers between devices: 248 us -> none  [the longest x1 190 us: shards(): pre_act = lax.psum(pre_part, 'mod')]
    all_gather x2 -> x0, waiting for transfers between devices: 149 us -> none  [carried_in(): gathered = jax.tree.map(lambda a: lax.all_gather(a, axis), part)]
    unnamed x6 -> x0, waiting for transfers between devices: 149 us -> none
    pallas_call x0 -> x5, Pallas kernels: none -> 141 us  [the longest x2 68.9 us: scan_call(): pl.pallas_call(functools.partial(scan_kernel, reverse), name='carry_rev'...]
    unnamed x1 -> x0, blocking collectives: 128 us -> none
    add x63 -> x0, other arithmetic: 66.4 us -> none  [merge_states(): following[0][:, None, None] * earlier[1] + following[1]]
    mul x63 -> x0, local copies, waits for them, and re-layouts: 43.9 us -> none  [merge_states(): following[0][:, None, None] * earlier[1] + following[1]]
    dot_general x20 -> x18, matrix products: 33 us -> 11.9 us  [ein(): return jnp.einsum(spec, *args, precision=high)]
  transfers between devices with their start and end apart: 5 -> 0, of which waited for: 5 -> 0; matrix products, arithmetic and copies ran while one was open for 3% -> 0% of each run, Pallas kernels for 0% -> 0%
where the time goes in v1:
time: 166 us; the launch traced here: 165 us
  Pallas kernels  141 us (85%)
  matrix products  11.9 us (7%)
  local copies, waits for them, and re-layouts  7.97 us (5%)
  other arithmetic  3.13 us (2%)
  between operations  1.72 us (1%)
    pallas_call x2, Pallas kernels, scan_call(): pl.pallas_call(functools.partial(scan_kernel, reverse), name='carry_rev'...  68.9 us
    pallas_call x1, Pallas kernels, grad_call(): pl.pallas_call(grad_kernel, name='weight_grads', out_shape=jax.ShapeDtype...  40.4 us
    pallas_call x2, Pallas kernels, sum_call(): pl.pallas_call(sum_kernel, name='sum_mod_%d' % cid, out_shape=jax.ShapeDt...  31.5 us
    dot_general x18, matrix products, ein(): return jnp.einsum(spec, *args, precision=high)  11.9 us

profile of v1, /device:TPU:1, one launch (start us, length us, event | category | flops | bytes accessed | tf_op | source)
XLA Modules:
  0.0 165.4 jit_solution(5588746019594073535)
XLA Ops:
  0.6 0.0 copy-start
  0.6 0.0 copy-start.1
  1.4 1.0 reduce_window_sum.11
  2.4 0.2 slice_reduce_fusion
  2.6 0.1 broadcast_select_fusion
  2.7 0.1 exponential_bitcast_fusion.1
  2.8 0.7 add.42.aux_ref
  3.5 1.1 fusion.60
  4.5 0.0 copy-done.1
  4.5 0.0 copy-start.8
  4.6 1.5 convolution_bitcast_fusion.4
  6.0 0.0 copy-done.8
  6.1 0.0 copy-start.5
  6.1 0.1 copy.23
  6.2 0.7 copy-done.5
  6.9 1.0 fusion.33.st_ref
  7.9 38.4 %carry_fwd.1 = (f32[8,64,128]{2,1,0:T(8,128)}, f32[8,8,128]{2,1,0:T(8,128)}) custom-call(f32[8,64,128]{2,1,0:T(8,128)} %fusion.33.st_ref, f32[8,8,128]{2,1,0:T(8,128)} %add.42.aux_ref), custom_call_target="tpu_custom_call" | custom-call | tf_op jit(solution)/shard_map/carry_fwd/pallas_call | solution.py:114
  46.3 0.0 copy-start.9
  46.3 0.6 copy-done.9
  46.9 0.0 copy-start.2
  46.9 0.0 copy-start.6
  46.9 0.7 fusion.2
  47.6 0.2 copy-done.2
  47.9 0.0 copy-done.6
  47.9 0.3 fusion.6
  48.2 0.0 copy-done
  48.2 0.4 fusion.10
  48.6 0.7 pad_maximum_fusion
  49.3 18.1 %sum_mod_2.1 = f32[8,16,512]{2,1,0:T(8,128)} custom-call(f32[8,16,512]{2,1,0:T(8,128)} %bitcast.107), custom_call_target="tpu_custom_call" | custom-call | tf_op jit(solution)/shard_map/sum_mod_2/pallas_call | solution.py:173
  67.4 1.0 fusion.57
  68.4 0.1 copy.43
  68.5 0.1 copy.42
  68.6 0.1 multiply_multiply_fusion
  68.7 0.4 convolution_add_fusion
  69.1 0.1 copy.28
  69.2 0.4 convolution_bitcast_fusion.5
  69.6 0.7 fusion
  70.3 0.2 convolution_add_fusion.2
  70.6 0.5 fusion.1
  71.1 1.0 fusion.30.st_ref
  72.0 30.5 %carry_rev.1 = (f32[8,64,128]{2,1,0:T(8,128)}, f32[8,8,128]{2,1,0:T(8,128)}) custom-call(f32[8,64,128]{2,1,0:T(8,128)} %fusion.30.st_ref, f32[8,8,128]{2,1,0:T(8,128)} %add.42.aux_ref), custom_call_target="tpu_custom_call" | custom-call | tf_op jit(solution)/shard_map/carry_rev/pallas_call | solution.py:114
  102.5 0.0 copy-start.3
  102.5 1.4 convolution_bitcast_fusion.6
  103.9 0.0 copy-done.3
  103.9 0.3 fusion.4
  104.2 0.2 convolution_add_fusion.3
  104.5 0.0 copy-start.4
  104.5 0.8 copy.29
  105.3 13.4 %sum_mod_5.1 = f32[8,16,256]{2,1,0:T(8,128)} custom-call(f32[8,16,256]{2,1,0:T(8,128)} %bitcast.109), custom_call_target="tpu_custom_call" | custom-call | tf_op jit(solution)/shard_map/sum_mod_5/pallas_call | solution.py:173
  118.6 0.0 copy-start.7
  118.6 0.8 copy.34
  119.5 0.1 copy-done.7
  119.5 0.7 fusion.58
  120.2 0.1 copy.26
  120.3 0.0 copy-done.4
  120.3 1.1 convolution_add_fusion.1
  121.4 0.4 fusion.46
  121.8 0.1 reshape.97
  121.9 0.4 fusion.35
  122.4 1.2 maximum_bitcast_fusion.g_ref
  123.6 40.4 %weight_grads.1 = f32[2,8,512]{2,1,0:T(8,128)} custom-call(f32[8,8,8,512]{3,2,1,0:T(8,128)} %maximum_bitcast_fusion.g_ref, f32[8,8,128]{2,1,0:T(8,128)} %get-tuple-element.11.lang_ref), custom_call_target="tpu_custom_call" | custom-call | tf_op jit(solution)/shard_map/weight_grads/pallas_call | solution.py:224
  164.0 1.5 fusion.59
  (4 shorter events, 0.1 us)
Async XLA Ops:
  0.6 47.5 %copy-start = (f32[2,512,256]{2,1,0:T(8,128)S(1)}, f32[2,512,256]{2,1,0:T(8,128)}, u32[]{:S(2)}) copy-start(f32[2,512,256]{2,1,0:T(8,128)} %param.14) | copy-start | bytes 3145732
  0.6 3.9 %copy-start.1 = (f32[128,512]{1,0:T(8,128)S(1)}, f32[128,512]{1,0:T(8,128)}, u32[]{:S(2)}) copy-start(f32[128,512]{1,0:T(8,128)} %param.17) | copy-start | bytes 786436
  4.5 1.5 copy-start.8
  6.1 0.8 copy-start.5
  46.3 0.7 copy-start.9
  46.9 0.9 copy-start.2
  46.9 1.0 copy-start.6
  102.5 1.4 copy-start.3
  104.5 15.9 %copy-start.4 = (f32[2,256,512]{2,1,0:T(8,128)S(1)}, f32[2,256,512]{2,1,0:T(8,128)}, u32[]{:S(2)}) copy-start(f32[2,256,512]{2,1,0:T(8,128)} %param.15) | copy-start | bytes 3145732
  118.6 0.9 copy-start.7

commit v2 on v0

v2 whole, which is shorter than its diff:
```python
import functools

import jax
import jax.numpy as jnp
from jax import lax
from jax.experimental import pallas as pl
from jax.experimental.pallas import tpu as pltpu
from jax.sharding import PartitionSpec as P

P_SIZE = 64
R = 256
LANG = 2
NY = 8
NZ = 8
NMOD = 8
f32 = jnp.float32
MESH = pl.DeviceIdType.MESH
high = lax.Precision.HIGH
VM = pl.BlockSpec(memory_space=pltpu.VMEM)
DMA = pltpu.SemaphoreType.DMA


def rcopy(src, dst, ss, rs, dev):
    return pltpu.make_async_remote_copy(
        src_ref=src, dst_ref=dst, send_sem=ss, recv_sem=rs, device_id=dev, device_id_type=MESH
    )


def ctx_place():
    c = lax.axis_index("ctx")
    return c // NY, c % NY, lax.axis_index("mod")


def y_dev(z, y, d):
    return {"ctx": z * NY + (y + d) % NY}


def z_dev(z, y, d):
    return {"ctx": ((z + d) % NZ) * NY + y}


def m_dev(m, d):
    return {"mod": (m + d) % NMOD}


def meet(z, y, m):
    barrier = pltpu.get_barrier_semaphore()
    for d in range(1, 8):
        for dev in (y_dev(z, y, d), z_dev(z, y, d), m_dev(m, d)):
            pl.semaphore_signal(barrier, inc=1, device_id=dev, device_id_type=MESH)
    pl.semaphore_wait(barrier, 21)


def dot3(a, b, ca, cb):
    def split(v):
        top = v.astype(jnp.bfloat16)
        return top, (v - top.astype(f32)).astype(jnp.bfloat16)

    def one(p, q):
        return lax.dot_general(p, q, (((ca,), (cb,)), ((), ())), preferred_element_type=f32)

    (ah, al), (bh, bl) = split(a), split(b)
    return one(ah, bh) + (one(ah, bl) + one(al, bh))


def send_all(pick, dst, ss, rs, dev):
    out = []
    for d in range(1, 8):
        cp = rcopy(pick(d), dst.at[d], ss.at[d], rs.at[d], dev(d))
        cp.start()
        out.append(cp)
    return out


def arrive(copies):
    for cp in copies:
        cp.wait_recv()


def add_up(own, copies, buf):
    total = own
    for d in range(1, 8):
        copies[d - 1].wait_recv()
        total = total + buf[d]
    return total


def row_prefix(reverse, y, gat, gaux, pre, pdec):
    state = jnp.zeros((P_SIZE, 128), f32)
    dec = jnp.ones((1, 128), f32)
    for s in range(NY - 1, -1, -1) if reverse else range(NY):
        slot = (y - s + NY) % NY
        pre[s] = state
        pdec[s] = jnp.broadcast_to(dec, (8, 128))
        dd = gaux[slot][0:1]
        state = dd * state + gat[slot]
        dec = dd * dec
    return state, dec


def row_carry(reverse, z, state_of, dec_of):
    carry = jnp.zeros((P_SIZE, 128), f32)
    for s in range(NZ - 1, -1, -1) if reverse else range(NZ):
        slot = (z - s + NZ) % NZ
        nxt = dec_of(slot) * carry + state_of(slot)
        use = (z < s) if reverse else (z > s)
        carry = jnp.where(use, nxt, carry)
    return carry


def fwd_kernel(
    st_ref, aux_ref, back_ref, hid_ref, head_ref, c_ref, down_ref,
    state_ref, auxy_ref, auxz_ref, hidden_ref, pre_ref, backsum_ref,
    gat, gaux, pre, pdec, tot, zg, ret, retin, part, rbuf, racc, rag, bbuf, bacc, bag,
    s1, r1, s2, r2, s3, r3, s4, r4, s5, r5, s6, r6, s7, r7, s8, r8,
):
    z, y, m = ctx_place()
    meet(z, y, m)
    ydev = lambda d: y_dev(z, y, d)
    zdev = lambda d: z_dev(z, y, d)
    mdev = lambda d: m_dev(m, d)
    c2 = send_all(lambda d: aux_ref.at[(y + d) % NY], gaux, s2, r2, ydev)
    c1 = send_all(lambda d: st_ref.at[(y + d) % NY], gat, s1, r1, ydev)
    c5 = send_all(lambda d: back_ref.at[(m + d) % NMOD], bbuf, s5, r5, mdev)
    gat[0] = st_ref[y]
    gaux[0] = aux_ref[y]
    arrive(c2 + c1)
    state, dec = row_prefix(False, y, gat, gaux, pre, pdec)
    tot[0:P_SIZE] = state
    lang_row = aux_ref[0][1:2]
    tot[P_SIZE:] = jnp.where(
        lax.broadcasted_iota(jnp.int32, (8, 128), 0) == 0,
        jnp.broadcast_to(dec, (8, 128)),
        jnp.broadcast_to(lang_row, (8, 128)),
    )
    c3 = send_all(lambda d: tot, zg, s3, r3, zdev)
    bacc[...] = add_up(back_ref[m], c5, bbuf)
    c6 = send_all(lambda d: bacc, bag, s6, r6, mdev)
    auxy_ref[...] = gaux[...]
    zg[0] = tot[...]
    arrive(c3)
    carry = row_carry(
        False, z, lambda i: zg[i, 0:P_SIZE], lambda i: zg[i, P_SIZE : P_SIZE + 8][0:1]
    )
    c4 = []
    for d in range(1, NY):
        s = (y + d) % NY
        ret[d] = pre[s] + pdec[s][0:1] * carry
        cp = rcopy(ret.at[d], retin.at[d], s4.at[d], r4.at[d], ydev(d))
        cp.start()
        c4.append(cp)
    retin[0] = pre[y] + pdec[y][0:1] * carry
    for d in range(NZ):
        auxz_ref[d] = zg[d, P_SIZE:]
    bag[0] = bacc[...]
    arrive(c6)
    for h in range(NMOD):
        backsum_ref[h] = bag[(m - h + NMOD) % NMOD]
    arrive(c4)
    for h in range(NY):
        state_ref[h] = retin[(y - h + NY) % NY]
    flat = state_ref[...].reshape(NY * P_SIZE, 128)
    hidden = hid_ref[...] + head_ref[...] * dot3(c_ref[...], flat, 1, 1)
    hidden_ref[...] = hidden
    part[...] = dot3(hidden, down_ref[...], 1, 0).reshape(NMOD, 16, R)
    c7 = send_all(lambda d: part.at[(m + d) % NMOD], rbuf, s7, r7, mdev)
    racc[...] = add_up(part[m], c7, rbuf)
    c8 = send_all(lambda d: racc, rag, s8, r8, mdev)
    rag[0] = racc[...]
    arrive(c8)
    for h in range(NMOD):
        pre_ref[h] = rag[(m - h + NMOD) % NMOD]
    for cp in c1 + c2 + c3 + c4 + c5 + c6 + c7 + c8:
        cp.wait_send()


def by_lang(buf, aux, out):
    def body(t, _):
        a, b = jnp.zeros((8, 256), f32), jnp.zeros((8, 256), f32)
        for d in range(8):
            v = buf[d, t]
            first = jnp.broadcast_to(aux[d][1:2, 0:1], (8, 256)) < 0.5
            a = a + jnp.where(first, v, 0.0)
            b = b + jnp.where(first, 0.0, v)
        out[t, 0] = a
        out[t, 1] = b
        return 0

    lax.fori_loop(0, 8, body, 0)


def bwd_kernel(
    st_ref, auxy_ref, auxz_ref, ga_ref, gb_ref, xt_ref, b_ref, c_ref,
    adj_ref, wa_ref, wb_ref, bsum_ref, csum_ref,
    gat, pre, pdec, tot, zg, ret, retin,
    abuf, apart, azbuf, zbuf, zpart, zybuf,
    cbuf, cacc, cag, part, rbuf, racc, rag,
    s1, r1, s3, r3, s4, r4, s5, r5, s6, r6, s7, r7, s8, r8,
    sa, ra, sb, rb, sc, rc, sd, rd, se, re, sf, rf,
):
    z, y, m = ctx_place()
    meet(z, y, m)
    ydev = lambda d: y_dev(z, y, d)
    zdev = lambda d: z_dev(z, y, d)
    mdev = lambda d: m_dev(m, d)

    def send_half(src, dst, place, half, ss, rs, dev):
        out = []
        for d in range(1, 8):
            cp = rcopy(
                src.at[(place + d) % 8, pl.ds(4 * half, 4)],
                dst.at[d, pl.ds(4 * half, 4)],
                ss.at[d], rs.at[d], dev(d),
            )
            cp.start()
            out.append(cp)
        return out

    c1 = send_all(lambda d: st_ref.at[(y + d) % NY], gat, s1, r1, ydev)
    c5 = send_all(lambda d: c_ref.at[(m + d) % NMOD], cbuf, s5, r5, mdev)
    cb0 = send_half(gb_ref, zbuf, z, 0, sc, rc, zdev)
    gat[0] = st_ref[y]
    arrive(c1)
    state, dec = row_prefix(True, y, gat, auxy_ref, pre, pdec)
    tot[...] = state
    c3 = send_all(lambda d: tot, zg, s3, r3, zdev)
    cb1 = send_half(gb_ref, zbuf, z, 1, sd, rd, zdev)
    ca0 = send_half(ga_ref, abuf, y, 0, sa, ra, ydev)
    cacc[...] = add_up(c_ref[m], c5, cbuf)
    c6 = send_all(lambda d: cacc, cag, s6, r6, mdev)
    zg[0] = tot[...]
    arrive(c3)
    carry = row_carry(True, z, lambda i: zg[i], lambda i: auxz_ref[i][0:1])
    c4 = []
    for d in range(1, NY):
        s = (y + d) % NY
        ret[d] = pre[s] + pdec[s][0:1] * carry
        cp = rcopy(ret.at[d], retin.at[d], s4.at[d], r4.at[d], ydev(d))
        cp.start()
        c4.append(cp)
    ca1 = send_half(ga_ref, abuf, y, 1, sb, rb, ydev)
    retin[0] = pre[y] + pdec[y][0:1] * carry
    abuf[0] = ga_ref[y]
    zbuf[0] = gb_ref[z]
    cag[0] = cacc[...]
    arrive(c6)
    for h in range(NMOD):
        csum_ref[h] = cag[(m - h + NMOD) % NMOD]
    arrive(c4)
    for h in range(NY):
        adj_ref[h] = retin[(y - h + NY) % NY]
    flat = adj_ref[...].reshape(NY * P_SIZE, 128)
    part[...] = (b_ref[...] + dot3(xt_ref[...], flat, 1, 0)).reshape(NMOD, 16, 128)
    c7 = send_all(lambda d: part.at[(m + d) % NMOD], rbuf, s7, r7, mdev)
    arrive(cb0 + cb1)
    by_lang(zbuf, auxz_ref, zpart)
    ce = send_all(lambda d: zpart.at[(y + d) % NY], zybuf, se, re, ydev)
    racc[...] = add_up(part[m], c7, rbuf)
    c8 = send_all(lambda d: racc, rag, s8, r8, mdev)
    arrive(ca0 + ca1)
    by_lang(abuf, auxy_ref, apart)
    cf = send_all(lambda d: apart.at[(z + d) % NZ], azbuf, sf, rf, zdev)
    rag[0] = racc[...]
    arrive(c8)
    for h in range(NMOD):
        bsum_ref[h] = rag[(m - h + NMOD) % NMOD]
    wb_ref[...] = add_up(zpart[y], ce, zybuf)
    wa_ref[...] = add_up(apart[z], cf, azbuf)
    for cp in c1 + c3 + c4 + c5 + c6 + c7 + c8 + ca0 + ca1 + cb0 + cb1 + ce + cf:
        cp.wait_send()


def vmem(*shape):
    return pltpu.VMEM(shape, f32)


def out_of(*shape):
    return jax.ShapeDtypeStruct(shape, f32)


def fwd_call(*args):
    chunk = (NMOD, 16, R)
    return pl.pallas_call(
        fwd_kernel,
        name="forward",
        out_shape=(
            out_of(8, P_SIZE, 128), out_of(8, 8, 128), out_of(8, 8, 128), out_of(128, 512),
            out_of(*chunk), out_of(*chunk),
        ),
        in_specs=[VM] * 7,
        out_specs=(VM,) * 6,
        scratch_shapes=[
            vmem(8, P_SIZE, 128), vmem(8, 8, 128), vmem(8, P_SIZE, 128), vmem(8, 8, 128),
            vmem(P_SIZE + 8, 128), vmem(8, P_SIZE + 8, 128),
            vmem(8, P_SIZE, 128), vmem(8, P_SIZE, 128),
            vmem(*chunk), vmem(*chunk), vmem(16, R), vmem(*chunk),
            vmem(*chunk), vmem(16, R), vmem(*chunk),
        ]
        + [DMA((8,))] * 16,
        compiler_params=pltpu.CompilerParams(collective_id=1, has_side_effects=True),
    )(*args)


def bwd_call(*args):
    chunk = (NMOD, 16, 128)
    big = (8, 8, 8, 256)
    mid = (8, LANG, 8, 256)
    return pl.pallas_call(
        bwd_kernel,
        name="backward",
        out_shape=(
            out_of(8, P_SIZE, 128), out_of(*mid[1:]), out_of(*mid[1:]), out_of(*chunk),
            out_of(*chunk),
        ),
        in_specs=[VM] * 8,
        out_specs=(VM,) * 5,
        scratch_shapes=[
            vmem(8, P_SIZE, 128), vmem(8, P_SIZE, 128), vmem(8, 8, 128),
            vmem(P_SIZE, 128), vmem(8, P_SIZE, 128),
            vmem(8, P_SIZE, 128), vmem(8, P_SIZE, 128),
            vmem(*big), vmem(*mid), vmem(*mid), vmem(*big), vmem(*mid), vmem(*mid),
            vmem(*chunk), vmem(16, 128), vmem(*chunk),
            vmem(*chunk), vmem(*chunk), vmem(16, 128), vmem(*chunk),
        ]
        + [DMA((8,))] * 26,
        compiler_params=pltpu.CompilerParams(collective_id=2, has_side_effects=True),
    )(*args)


def ein(spec, *args):
    return jnp.einsum(spec, *args, precision=high)


def shards(
    seq_input, log_decay, b_proj, c_proj, skip_gain, down_weight, up_weight, block_lang, cotangent
):
    rows, width = seq_input.shape
    heads = log_decay.shape[0]
    x = seq_input.reshape(rows, heads, P_SIZE)
    cumulative = jnp.cumsum(log_decay, axis=1)
    lower = jnp.tril(jnp.ones((rows, rows), bool))
    gaps = cumulative[:, :, None] - cumulative[:, None, :]
    decay_mask = jnp.where(lower, jnp.exp(jnp.where(lower, gaps, 0.0)), 0.0)
    mixing = decay_mask * ein("tn,sn->ts", c_proj, b_proj)
    tail = jnp.exp(cumulative[:, -1:] - cumulative)
    total = jnp.exp(cumulative[:, -1])
    head = jnp.exp(cumulative)
    lang = block_lang[0]
    down = lax.dynamic_index_in_dim(down_weight, lang, 0, False)
    up = lax.dynamic_index_in_dim(up_weight, lang, 0, False)

    aux = jnp.where(
        jnp.arange(8)[None, :, None] == 0, total[:, None, None], lang.astype(f32)
    ) + jnp.zeros((heads, 8, 128), f32)
    local_state = ein("shp,sn->hpn", tail.T[:, :, None] * x, b_proj)
    head_full = jnp.repeat(head.T, P_SIZE, axis=1)
    back_part = ein("tf,rf->tr", cotangent, up)
    hid = ein("hts,shp->thp", mixing, x) + skip_gain[None, :, None] * x
    chunk = (NMOD, rows // NMOD, -1)
    state_in, aux_y, aux_z, hidden, pre_sum, back_sum = fwd_call(
        local_state, aux, back_part.reshape(chunk), hid.reshape(rows, width), head_full,
        c_proj, down,
    )
    pre_act, back_act = pre_sum.reshape(rows, R), back_sum.reshape(rows, R)
    gate = jax.nn.sigmoid(pre_act)
    active = pre_act * gate
    pre_grad = back_act * (gate * (1.0 + pre_act * (1.0 - gate)))
    hidden_grad = cotangent + ein("tr,fr->tf", pre_grad, down)
    gh = hidden_grad.reshape(rows, heads, P_SIZE)
    local_adjoint = ein("shp,sn->hpn", head.T[:, :, None] * gh, c_proj)
    layer_out = hidden + ein("tr,rf->tf", active, up)
    down_t = ein("tr,tf->rf", pre_grad, hidden).reshape(NZ, NY, 4, width)
    up_t = ein("tr,tf->rf", active, cotangent).reshape(NZ, NY, 4, width)
    g = jnp.concatenate([down_t, up_t], axis=2)
    half = width // 2
    weighted = jnp.sum(decay_mask * ein("thp,shp->hts", gh, x), axis=0)
    b_part = ein("ts,tn->sn", weighted, c_proj)
    c_part = ein("ts,sn->tn", weighted, b_proj)
    c_part = c_part + ein("thp,hpn->tn", head.T[:, :, None] * gh, state_in)
    xt = (tail.T[:, :, None] * x).reshape(rows, width)
    adjoint_in, wa, wb, b_sum, c_sum = bwd_call(
        local_adjoint, aux_y, aux_z, g[..., :half].transpose(1, 0, 2, 3), g[..., half:],
        xt, b_part, c_part.reshape(chunk),
    )
    wg = jnp.concatenate([wa, wb], axis=2)
    input_grad = ein("hts,thp->shp", mixing, gh) + skip_gain[None, :, None] * gh
    input_grad = input_grad + tail.T[:, :, None] * ein("hpn,sn->shp", adjoint_in, b_proj)
    return (
        layer_out,
        input_grad.reshape(rows, width),
        b_sum.reshape(rows, 128),
        c_sum.reshape(rows, 128),
        wg[:, :4].transpose(0, 2, 1),
        wg[:, 4:],
    )


def solution(mesh):
    return jax.shard_map(
        shards,
        mesh=mesh,
        in_specs=(
            P("ctx", "mod"),
            P("mod", "ctx"),
            P("ctx", None),
            P("ctx", None),
            P("mod"),
            P(None, "mod", None),
            P(None, None, "mod"),
            P("ctx"),
            P("ctx", "mod"),
        ),
        out_specs=(
            P("ctx", "mod"),
            P("ctx", "mod"),
            P("ctx", None),
            P("ctx", None),
            P(None, "mod", "ctx"),
            P(None, "ctx", "mod"),
        ),
        check_vma=False,
    )
```

time: 860 us -> 132 us (0.15)
  waiting for transfers between devices: 546 us -> 0 us
  blocking collectives: 128 us -> 0 us
  Pallas kernels: 0 us -> 100 us
  other arithmetic: 69.5 us -> 4.77 us
  local copies, waits for them, and re-layouts: 59.7 us -> 15.2 us
  matrix products: 33 us -> 9.62 us
  between operations: 16 us -> 1.55 us
    psum x2 -> x0, waiting for transfers between devices: 248 us -> none  [the longest x1 190 us: shards(): pre_act = lax.psum(pre_part, 'mod')]
    all_gather x2 -> x0, waiting for transfers between devices: 149 us -> none  [carried_in(): gathered = jax.tree.map(lambda a: lax.all_gather(a, axis), part)]
    unnamed x6 -> x0, waiting for transfers between devices: 149 us -> none
    unnamed x1 -> x0, blocking collectives: 128 us -> none
    pallas_call x0 -> x2, Pallas kernels: none -> 100 us  [the longest x1 50.4 us: fwd_call(): pl.pallas_call(fwd_kernel, name='forward', out_shape=(out_of(8, P_SIZE, 1...]
    add x63 -> x0, other arithmetic: 66.4 us -> none  [merge_states(): following[0][:, None, None] * earlier[1] + following[1]]
    mul x63 -> x2, local copies, waits for them, and re-layouts: 43.9 us -> 0.15 us  [shards(): local_state = ein('shp,sn->hpn', tail.T[:, :, None] * x, b_proj)]
    dot_general x20 -> x15, matrix products: 33 us -> 9.62 us  [ein(): return jnp.einsum(spec, *args, precision=high)]
  transfers between devices with their start and end apart: 5 -> 0, of which waited for: 5 -> 0; matrix products, arithmetic and copies ran while one was open for 3% -> 0% of each run, Pallas kernels for 0% -> 0%
where the time goes in v2:
time: 132 us; the launch traced here: 131 us
  Pallas kernels  100 us (76%)
  local copies, waits for them, and re-layouts  15.2 us (12%)
  matrix products  9.62 us (7%)
  other arithmetic  4.77 us (4%)
  between operations  1.55 us (1%)
    pallas_call x1, Pallas kernels, fwd_call(): pl.pallas_call(fwd_kernel, name='forward', out_shape=(out_of(8, P_SIZE, 1...  50.4 us
    pallas_call x1, Pallas kernels, bwd_call(): pl.pallas_call(bwd_kernel, name='backward', out_shape=(out_of(8, P_SIZE,...  49.7 us
    dot_general x15, matrix products, ein(): return jnp.einsum(spec, *args, precision=high)  9.62 us
    unnamed x49, local copies, waits for them, and re-layouts  9.26 us

profile of v2, /device:TPU:1, one launch (start us, length us, event | category | flops | bytes accessed | tf_op | source)
XLA Modules:
  0.0 131.3 jit_solution(2717273444889368850)
XLA Ops:
  0.6 0.0 copy-start
  0.6 1.1 reduce_window_sum.11
  1.7 0.2 slice_reduce_fusion
  1.9 0.1 exponential_bitcast_fusion
  2.0 1.1 copy.24
  3.1 0.0 copy-done.8
  3.1 1.0 fusion.27.st_ref
  4.1 0.8 copy.26.head_ref
  5.6 0.0 copy-done
  5.6 0.0 copy-start.2
  5.6 0.8 dynamic-slice_bitcast_fusion.down_ref
  6.4 0.1 copy-done.2
  6.6 1.1 fusion.8
  7.7 0.0 copy-start.21
  7.7 0.2 fusion.47
  7.9 0.4 copy-done.17
  8.2 0.1 copy-done.21
  8.3 0.7 fusion.2
  9.0 0.8 copy.25.hid_ref
  9.9 0.1 broadcast_select_fusion
  9.9 0.7 add.42.aux_ref
  10.6 50.4 %forward.1 = (f32[8,64,128]{2,1,0:T(8,128)}, f32[8,8,128]{2,1,0:T(8,128)}, f32[8,8,128]{2,1,0:T(8,128)}, f32[128,512]{1,0:T(8,128)}, f32[8,16,256]{2,1,0:T(8,128)}, /*index=5*/f32[8,16,256]{2,1,0:T(8,128)}) custom-call(f32[8,64,128]{2,1,0:T(8,128)} %fusion.27.st_ref, f32[8,8,128]{2,1,0:T(8,128)} %add.42.aux_ref, f32[8,16,256]{2,1,0:T(8,128)} %bitcast.104, ...), custom_call_target="tpu_custom_call" | custom-call | tf_op jit(solution)/shard_map/forward/pallas_call | solution.py:283
  61.0 1.7 %multiply_multiply_fusion.1 = (f32[8,16,256]{2,1,0:T(8,128)S(1)}, f32[8,16,256]{2,1,0:T(8,128)}) fusion(f32[8,16,256]{2,1,0:T(8,128)} %get-tuple-element.19, f32[8,16,256]{2,1,0:T(8,128)} %get-tuple-element.18), kind=kLoop, calls=%fused_computation.48 | loop fusion | flops 294912 | bytes 524288 | tf_op jit(solution)/shard_map/mul | solution.py:367
  62.8 0.4 convolution_add_fusion
  63.2 0.0 copy-start.13
  63.2 0.1 copy.27
  63.3 0.8 copy-done.13
  64.1 0.4 convolution_bitcast_fusion.3
  64.5 0.3 copy-done.18
  64.9 0.7 fusion
  65.5 0.8 convolution_add_fusion.2
  66.3 0.1 copy-done.11
  66.4 0.8 copy.28
  67.2 0.1 copy-done.10
  67.3 0.1 copy.30
  67.4 0.8 copy-done.12
  68.2 0.1 fusion.34
  68.3 0.9 copy-done.7
  69.2 0.4 fusion.17
  69.6 0.4 fusion.15
  70.0 1.0 pad_maximum_fusion
  71.1 0.8 copy.37.ga_ref
  71.9 0.0 copy-done.4
  71.9 0.9 fusion.48.b_ref
  72.8 1.0 fusion.32.st_ref
  73.8 0.0 copy-start.5
  73.8 0.1 copy.36
  73.9 0.8 copy-done.5
  74.7 0.7 mul.105.xt_ref
  75.5 49.7 %backward.1 = (f32[8,64,128]{2,1,0:T(8,128)}, f32[2,8,256]{2,1,0:T(8,128)}, f32[2,8,256]{2,1,0:T(8,128)}, f32[8,16,128]{2,1,0:T(8,128)}, f32[8,16,128]{2,1,0:T(8,128)}) custom-call(f32[8,64,128]{2,1,0:T(8,128)} %fusion.32.st_ref, f32[8,8,128]{2,1,0:T(8,128)} %get-tuple-element.20.auxy_ref, f32[8,8,128]{2,1,0:T(8,128)} %get-tuple-element.21.auxz_ref, ...), custom_call_target="tpu_custom_call" | custom-call | tf_op jit(solution)/shard_map/backward/pallas_call | solution.py:308
  125.2 0.7 constant_dynamic-update-slice_fusion.1
  125.9 0.0 copy-done.20
  125.9 0.6 fusion.46
  126.6 0.1 copy-done.19
  126.6 0.5 fusion.1
  127.1 0.5 copy-done.14
  127.6 0.3 fusion.4
  127.9 0.0 copy-start.9
  127.9 0.8 copy.38
  128.7 0.1 copy-done.9
  128.8 1.0 convolution_add_fusion.1
  129.8 0.6 copy.49
  130.4 0.2 copy-done.15
  130.7 0.6 copy.50
  (26 shorter events, 0.1 us)
Async XLA Ops:
  0.6 4.9 %copy-start = (f32[2,512,256]{2,1,0:T(8,128)S(1)}, f32[2,512,256]{2,1,0:T(8,128)}, u32[]{:S(2)}) copy-start(f32[2,512,256]{2,1,0:T(8,128)} %param.14) | copy-start | bytes 3145732
  2.0 1.1 copy-start.8
  4.0 2.4 %copy-start.6 = (f32[2,256,512]{2,1,0:T(8,128)S(1)}, f32[2,256,512]{2,1,0:T(8,128)}, u32[]{:S(2)}) copy-start(f32[2,256,512]{2,1,0:T(8,128)} %param.15) | copy-start | bytes 3145732
  5.6 1.0 copy-start.2
  6.6 1.1 copy-start.3
  7.6 0.6 copy-start.17
  7.7 0.7 copy-start.21
  61.0 1.8 %copy-start.1 = (f32[512,256]{1,0:T(8,128)S(1)}, f32[512,256]{1,0:T(8,128)}, u32[]{:S(2)}) copy-start(f32[512,256]{1,0:T(8,128)} %dynamic-slice_bitcast_fusion.down_ref) | copy-start | bytes 1572868
  63.2 1.0 copy-start.13
  64.1 0.7 copy-start.18
  65.5 0.9 copy-start.11
  66.4 0.9 copy-start.10
  67.3 0.9 copy-start.12
  68.2 0.9 copy-start.7
  71.0 0.8 copy-start.4
  73.8 1.0 copy-start.5
  125.2 0.7 copy-start.20
  125.9 0.7 copy-start.19
  126.6 0.9 copy-start.14
  127.9 0.9 copy-start.9
  128.8 1.0 copy-start.16
  129.8 0.9 copy-start.15

commit v3 on v0

v3 whole, which is shorter than its diff:
```python
import jax
import jax.numpy as jnp
from jax import lax
from jax.experimental import pallas as pl
from jax.experimental.pallas import tpu as pltpu
from jax.sharding import PartitionSpec as P

P_SIZE = 64
R = 256
LANG = 2
NY = 8
NZ = 8
NMOD = 8
f32 = jnp.float32
MESH = pl.DeviceIdType.MESH
VM = pl.BlockSpec(memory_space=pltpu.VMEM)
DMA = pltpu.SemaphoreType.DMA


def rcopy(src, dst, ss, rs, dev):
    return pltpu.make_async_remote_copy(
        src_ref=src, dst_ref=dst, send_sem=ss, recv_sem=rs, device_id=dev, device_id_type=MESH
    )


def ctx_place():
    c = lax.axis_index("ctx")
    return c // NY, c % NY, lax.axis_index("mod")


def y_dev(z, y, d):
    return {"ctx": z * NY + (y + d) % NY}


def z_dev(z, y, d):
    return {"ctx": ((z + d) % NZ) * NY + y}


def m_dev(m, d):
    return {"mod": (m + d) % NMOD}


def greet(z, y, m):
    barrier = pltpu.get_barrier_semaphore()
    for d in range(1, 8):
        for dev in (y_dev(z, y, d), z_dev(z, y, d), m_dev(m, d)):
            pl.semaphore_signal(barrier, inc=1, device_id=dev, device_id_type=MESH)


def dot3(a, b, ca, cb):
    def split(v):
        top = v.astype(jnp.bfloat16)
        return top, (v - top.astype(f32)).astype(jnp.bfloat16)

    def one(p, q):
        return lax.dot_general(p, q, (((ca,), (cb,)), ((), ())), preferred_element_type=f32)

    (ah, al), (bh, bl) = split(a), split(b)
    return one(ah, bh) + (one(ah, bl) + one(al, bh))


def send_all(pick, dst, ss, rs, dev):
    out = []
    for d in range(1, 8):
        cp = rcopy(pick(d), dst.at[d], ss.at[d], rs.at[d], dev(d))
        cp.start()
        out.append(cp)
    return out


def arrive(copies):
    for cp in copies:
        cp.wait_recv()


def add_up(own, copies, buf):
    total = own
    for d in range(1, 8):
        copies[d - 1].wait_recv()
        total = total + buf[d]
    return total


def row_prefix(reverse, y, gat, gaux, pre, pdec):
    state = jnp.zeros((P_SIZE, 128), f32)
    dec = jnp.ones((1, 128), f32)
    for s in range(NY - 1, -1, -1) if reverse else range(NY):
        slot = (y - s + NY) % NY
        pre[s] = state
        pdec[s] = jnp.broadcast_to(dec, (8, 128))
        dd = gaux[slot][0:1]
        state = dd * state + gat[slot]
        dec = dd * dec
    return state, dec


def row_carry(reverse, z, state_of, dec_of):
    carry = jnp.zeros((P_SIZE, 128), f32)
    for s in range(NZ - 1, -1, -1) if reverse else range(NZ):
        slot = (z - s + NZ) % NZ
        nxt = dec_of(slot) * carry + state_of(slot)
        use = (z < s) if reverse else (z > s)
        carry = jnp.where(use, nxt, carry)
    return carry


def by_lang(buf, aux, out):
    def body(t, _):
        a, b = jnp.zeros((8, 256), f32), jnp.zeros((8, 256), f32)
        for d in range(8):
            v = buf[d, t]
            first = jnp.broadcast_to(aux[d][1:2, 0:1], (8, 256)) < 0.5
            a = a + jnp.where(first, v, 0.0)
            b = b + jnp.where(first, 0.0, v)
        out[t, 0] = a
        out[t, 1] = b
        return 0

    lax.fori_loop(0, 8, body, 0)


def layer_kernel(
    lang_ref, x_ref, ld_ref, b_ref, c_ref, skip_ref, down_ref, up_ref, cot_ref,
    out_ref, ig_ref, bsum_ref, csum_ref, downg_ref, upg_ref,
    st, aux, gat, gaux, pre, pdec, tot, zg, ret, retin,
    back, bbuf, bacc, bag, part, rbuf, racc, rag,
    st2, gat2, tot2, zg2, ret2, retin2,
    g, abuf, apart, azbuf, zbuf, zpart, zybuf, auxz,
    cpart, cbuf, cacc, cag, bpart, xbuf, xacc, xag,
    mix, dmask, hid, headf, tailf, ghs, wg,
    s1, r1, s2, r2, s3, r3, s4, r4, s5, r5, s6, r6, s7, r7, s8, r8,
    t1, q1, t3, q3, t4, q4, t5, q5, t6, q6, t7, q7, t8, q8,
    sa, ra, sb, rb, sc, rc, sd, rd, se, re, sf, rf,
):
    z, y, m = ctx_place()
    greet(z, y, m)
    ydev = lambda d: y_dev(z, y, d)
    zdev = lambda d: z_dev(z, y, d)
    mdev = lambda d: m_dev(m, d)
    lang = lang_ref[0]
    iota = lambda shape, dim: lax.broadcasted_iota(jnp.int32, shape, dim)
    sq = (128, 128)
    lower = iota(sq, 0) >= iota(sq, 1)
    left = iota(sq, 1) < P_SIZE
    pairs = [slice(128 * p, 128 * p + 128) for p in range(4)]

    def spread(v, p):
        return jnp.where(
            left,
            jnp.broadcast_to(v[:, 2 * p : 2 * p + 1], sq),
            jnp.broadcast_to(v[:, 2 * p + 1 : 2 * p + 2], sq),
        )

    ones = lower.astype(f32)
    ld = ld_ref[...]
    full = lax.Precision.HIGHEST
    cum_row = lax.dot_general(
        ld, ones, (((1,), (1,)), ((), ())), precision=full, preferred_element_type=f32
    )
    cum_col = lax.dot_general(
        ones, ld, (((1,), (1,)), ((), ())), precision=full, preferred_element_type=f32
    )
    tail_c = jnp.exp(cum_col[127:128, :] - cum_col)
    head_c = jnp.exp(cum_col)
    for p in range(4):
        tailf[:, pairs[p]] = spread(tail_c, p)
        headf[:, pairs[p]] = spread(head_c, p)
    b, c = b_ref[...], c_ref[...]
    st[...] = dot3(tailf[...] * x_ref[...], b, 0, 0).reshape(8, P_SIZE, 128)
    total = jnp.exp(cum_row[:, 127:128])
    lang_tile = jnp.full((8, 128), lang.astype(f32), f32)
    top_row = iota((8, 128), 0) == 0
    for h in range(8):
        aux[h] = jnp.where(top_row, jnp.broadcast_to(total[h : h + 1, :], (8, 128)), lang_tile)
    pl.semaphore_wait(pltpu.get_barrier_semaphore(), 21)

    c2 = send_all(lambda d: aux.at[(y + d) % NY], gaux, s2, r2, ydev)
    c1 = send_all(lambda d: st.at[(y + d) % NY], gat, s1, r1, ydev)
    gat[0] = st[y]
    gaux[0] = aux[y]
    back[...] = dot3(cot_ref[...], up_ref[lang], 1, 1).reshape(NMOD, 16, R)
    c5 = send_all(lambda d: back.at[(m + d) % NMOD], bbuf, s5, r5, mdev)
    scores = dot3(c, b, 1, 1)
    for p in range(4):
        xp = x_ref[:, pairs[p]]
        got = []
        for h in (2 * p, 2 * p + 1):
            gap = jnp.broadcast_to(cum_col[:, h : h + 1], sq) - jnp.broadcast_to(
                cum_row[h : h + 1, :], sq
            )
            dm = jnp.where(lower, jnp.exp(jnp.where(lower, gap, 0.0)), 0.0)
            dmask[h] = dm
            mix[h] = dm * scores
            got.append(dot3(mix[h], xp, 1, 0))
        hid[:, pairs[p]] = jnp.where(left, got[0], got[1]) + skip_ref[:, pairs[p]] * xp
    arrive(c2 + c1)
    state, dec = row_prefix(False, y, gat, gaux, pre, pdec)
    tot[0:P_SIZE] = state
    tot[P_SIZE:] = jnp.where(top_row, jnp.broadcast_to(dec, (8, 128)), lang_tile)
    c3 = send_all(lambda d: tot, zg, s3, r3, zdev)
    bacc[...] = add_up(back[m], c5, bbuf)
    c6 = send_all(lambda d: bacc, bag, s6, r6, mdev)
    zg[0] = tot[...]
    bag[0] = bacc[...]
    arrive(c3)
    carry = row_carry(
        False, z, lambda i: zg[i, 0:P_SIZE], lambda i: zg[i, P_SIZE : P_SIZE + 8][0:1]
    )

    def send_back(pre, carry, ret, retin, ss, rs):
        out = []
        for d in range(1, NY):
            s = (y + d) % NY
            ret[d] = pre[s] + pdec[s][0:1] * carry
            cp = rcopy(ret.at[d], retin.at[d], ss.at[d], rs.at[d], ydev(d))
            cp.start()
            out.append(cp)
        retin[0] = pre[y] + pdec[y][0:1] * carry
        return out

    def in_order(buf, place):
        return jnp.concatenate([buf[(place - h + 8) % 8] for h in range(8)], axis=0)

    c4 = send_back(pre, carry, ret, retin, s4, r4)
    for d in range(NZ):
        auxz[d] = zg[d, P_SIZE:]
    arrive(c6)
    back_act = in_order(bag, m)
    arrive(c4)
    state_in = in_order(retin, y)
    hid[...] = hid[...] + headf[...] * dot3(c, state_in, 1, 1)
    part[...] = dot3(hid[...], down_ref[lang], 1, 0).reshape(NMOD, 16, R)
    c7 = send_all(lambda d: part.at[(m + d) % NMOD], rbuf, s7, r7, mdev)
    racc[...] = add_up(part[m], c7, rbuf)
    c8 = send_all(lambda d: racc, rag, s8, r8, mdev)
    rag[0] = racc[...]
    arrive(c8)
    pre_act = in_order(rag, m)
    gate = jax.nn.sigmoid(pre_act)
    active = pre_act * gate
    pre_grad = back_act * (gate * (1.0 + pre_act * (1.0 - gate)))

    gh = cot_ref[...] + dot3(pre_grad, down_ref[lang], 1, 1)
    ghs[...] = gh
    head_gh = headf[...] * gh
    st2[...] = dot3(head_gh, c, 0, 0).reshape(8, P_SIZE, 128)
    e1 = send_all(lambda d: st2.at[(y + d) % NY], gat2, t1, q1, ydev)
    gat2[0] = st2[y]

    col = iota((R, 2 * R), 1)
    pick = (iota((R, 2 * R), 0) == 4 * (col // 8) + col % 4).astype(f32)
    both = jnp.where(
        iota((128, 2 * R), 1) % 8 < 4, dot3(pre_grad, pick, 1, 0), dot3(active, pick, 1, 0)
    )
    from_down = iota((2 * R, 256), 0) % 8 < 4
    for half in (1, 0):
        lanes = slice(256 * half, 256 * half + 256)
        g[half] = jnp.where(
            from_down,
            dot3(both, hid[:, lanes], 0, 0),
            dot3(both, cot_ref[:, lanes], 0, 0),
        ).reshape(NZ, NY, 8, 256)

    def send_half(z_first, half, ss, rs):
        out = []
        dst = zbuf if z_first else abuf
        for d in range(1, 8):
            if z_first:
                src = g.at[1, (z + d) % NZ, pl.ds(4 * half, 4)]
            else:
                src = g.at[0, pl.ds(4 * half, 4), (y + d) % NY]
            cp = rcopy(
                src, dst.at[d, pl.ds(4 * half, 4)], ss.at[d], rs.at[d],
                zdev(d) if z_first else ydev(d),
            )
            cp.start()
            out.append(cp)
        return out

    cb0 = send_half(True, 0, sc, rc)
    weighted = jnp.zeros(sq, f32)
    for p in range(4):
        xp, gp = x_ref[:, pairs[p]], ghs[:, pairs[p]]
        weighted = weighted + dmask[2 * p] * dot3(jnp.where(left, gp, 0.0), xp, 1, 1)
        weighted = weighted + dmask[2 * p + 1] * dot3(jnp.where(left, 0.0, gp), xp, 1, 1)
    cpart[...] = (dot3(weighted, b, 1, 0) + dot3(head_gh, state_in, 1, 0)).reshape(8, 16, 128)
    e5 = send_all(lambda d: cpart.at[(m + d) % NMOD], cbuf, t5, q5, mdev)
    arrive(e1)
    state, _ = row_prefix(True, y, gat2, gaux, pre, pdec)
    tot2[...] = state
    e3 = send_all(lambda d: tot2, zg2, t3, q3, zdev)
    cb1 = send_half(True, 1, sd, rd)
    ca0 = send_half(False, 0, sa, ra)
    zg2[0] = tot2[...]
    cacc[...] = add_up(cpart[m], e5, cbuf)
    e6 = send_all(lambda d: cacc, cag, t6, q6, mdev)
    out_ref[...] = hid[...] + dot3(active, up_ref[lang], 1, 0)
    b_part = dot3(weighted, c, 0, 0)
    arrive(e3)
    carry = row_carry(True, z, lambda i: zg2[i], lambda i: auxz[i][0:1])
    e4 = send_back(pre, carry, ret2, retin2, t4, q4)
    ca1 = send_half(False, 1, sb, rb)
    zbuf[0] = g[1, z]
    for t in range(NZ):
        abuf[0, t] = g[0, t, y]
    cag[0] = cacc[...]
    for p in range(4):
        gp = ghs[:, pairs[p]]
        ig_ref[:, pairs[p]] = (
            jnp.where(left, dot3(mix[2 * p], gp, 0, 0), dot3(mix[2 * p + 1], gp, 0, 0))
            + skip_ref[:, pairs[p]] * gp
        )
    arrive(e6)
    csum_ref[...] = in_order(cag, m)
    arrive(e4)
    adj = in_order(retin2, y)
    bpart[...] = (b_part + dot3(tailf[...] * x_ref[...], adj, 1, 0)).reshape(8, 16, 128)
    e7 = send_all(lambda d: bpart.at[(m + d) % NMOD], xbuf, t7, q7, mdev)
    ig_ref[...] = ig_ref[...] + tailf[...] * dot3(b, adj, 1, 1)
    xacc[...] = add_up(bpart[m], e7, xbuf)
    e8 = send_all(lambda d: xacc, xag, t8, q8, mdev)
    xag[0] = xacc[...]
    arrive(cb0 + cb1)
    by_lang(zbuf, auxz, zpart)
    ce = send_all(lambda d: zpart.at[(y + d) % NY], zybuf, se, re, ydev)
    arrive(ca0 + ca1)
    by_lang(abuf, gaux, apart)
    cf = send_all(lambda d: apart.at[(z + d) % NZ], azbuf, sf, rf, zdev)
    arrive(e8)
    bsum_ref[...] = in_order(xag, m)
    wg[:, :, 256:] = add_up(zpart[y], ce, zybuf)
    wg[:, :, :256] = add_up(apart[z], cf, azbuf)
    downg_ref[...] = wg[:, 0:4, :]
    upg_ref[...] = wg[:, 4:8, :]
    for cp in c1 + c2 + c3 + c4 + c5 + c6 + c7 + c8 + e1 + e3 + e4 + e5 + e6 + e7 + e8:
        cp.wait_send()
    for cp in ca0 + ca1 + cb0 + cb1 + ce + cf:
        cp.wait_send()


def vmem(*shape):
    return pltpu.VMEM(shape, f32)


def out_of(*shape):
    return jax.ShapeDtypeStruct(shape, f32)


def layer_call(*args):
    st, tile, wide = (8, P_SIZE, 128), (8, 8, 128), (128, 512)
    act, proj = (8, 16, R), (8, 16, 128)
    big, mid = (8, 8, 8, 256), (8, LANG, 8, 256)
    shapes = [
        st, tile, st, tile, st, tile, (P_SIZE + 8, 128), (8, P_SIZE + 8, 128), st, st,
        act, act, act[1:], act, act, act, act[1:], act,
        st, st, st[1:], st, st, st,
        (2,) + big, big, mid, mid, big, mid, mid, tile,
        proj, proj, proj[1:], proj, proj, proj, proj[1:], proj,
        (8, 128, 128), (8, 128, 128), wide, wide, wide, wide, (LANG, 8, 512),
    ]
    return pl.pallas_call(
        layer_kernel,
        name="layer",
        out_shape=(
            out_of(*wide), out_of(*wide), out_of(128, 128), out_of(128, 128),
            out_of(LANG, 4, 512), out_of(LANG, 4, 512),
        ),
        in_specs=[pl.BlockSpec(memory_space=pltpu.SMEM)] + [VM] * 8,
        out_specs=(VM,) * 6,
        scratch_shapes=[vmem(*s) for s in shapes] + [DMA((8,))] * 42,
        compiler_params=pltpu.CompilerParams(collective_id=1, has_side_effects=True),
    )(*args)


def shards(
    seq_input, log_decay, b_proj, c_proj, skip_gain, down_weight, up_weight, block_lang, cotangent
):
    skip = jnp.repeat(skip_gain, P_SIZE)[None, :]
    layer_out, input_grad, b_grad, c_grad, down_t, up_grad = layer_call(
        block_lang, seq_input, log_decay, b_proj, c_proj, skip, down_weight, up_weight, cotangent
    )
    return layer_out, input_grad, b_grad, c_grad, down_t.transpose(0, 2, 1), up_grad


def solution(mesh):
    return jax.shard_map(
        shards,
        mesh=mesh,
        in_specs=(
            P("ctx", "mod"),
            P("mod", "ctx"),
            P("ctx", None),
            P("ctx", None),
            P("mod"),
            P(None, "mod", None),
            P(None, None, "mod"),
            P("ctx"),
            P("ctx", "mod"),
        ),
        out_specs=(
            P("ctx", "mod"),
            P("ctx", "mod"),
            P("ctx", None),
            P("ctx", None),
            P(None, "mod", "ctx"),
            P(None, "ctx", "mod"),
        ),
        check_vma=False,
    )
```

time: 860 us -> 104 us (0.12)
  waiting for transfers between devices: 546 us -> 0 us
  blocking collectives: 128 us -> 0 us
  Pallas kernels: 0 us -> 95.9 us
  other arithmetic: 69.5 us -> 0 us
  local copies, waits for them, and re-layouts: 59.7 us -> 6.22 us
  matrix products: 33 us -> 0 us
  between operations: 16 us -> 1.33 us
    psum x2 -> x0, waiting for transfers between devices: 248 us -> none  [the longest x1 190 us: shards(): pre_act = lax.psum(pre_part, 'mod')]
    all_gather x2 -> x0, waiting for transfers between devices: 149 us -> none  [carried_in(): gathered = jax.tree.map(lambda a: lax.all_gather(a, axis), part)]
    unnamed x6 -> x0, waiting for transfers between devices: 149 us -> none
    unnamed x1 -> x0, blocking collectives: 128 us -> none
    pallas_call x0 -> x1, Pallas kernels: none -> 95.9 us  [layer_call(): pl.pallas_call(layer_kernel, name='layer', out_shape=(out_of(*wide), out_...]
    add x63 -> x0, other arithmetic: 66.4 us -> none  [merge_states(): following[0][:, None, None] * earlier[1] + following[1]]
    mul x63 -> x0, local copies, waits for them, and re-layouts: 43.9 us -> none  [merge_states(): following[0][:, None, None] * earlier[1] + following[1]]
    dot_general x20 -> x0, matrix products: 33 us -> none  [the longest x1 3.04 us: shards(): jnp.dot(spread.T, cotangent, precision=highest).reshape(LANG, R, width)]
  transfers between devices with their start and end apart: 5 -> 0, of which waited for: 5 -> 0; matrix products, arithmetic and copies ran while one was open for 3% -> 0% of each run, Pallas kernels for 0% -> 0%
where the time goes in v3:
time: 104 us; the launch traced here: 103 us
  Pallas kernels  95.9 us (92%)
  local copies, waits for them, and re-layouts  6.22 us (6%)
  between operations  1.33 us (1%)
    pallas_call x1, Pallas kernels, layer_call(): pl.pallas_call(layer_kernel, name='layer', out_shape=(out_of(*wide), out_...  95.9 us
    unnamed x18, local copies, waits for them, and re-layouts  5.49 us

profile of v3, /device:TPU:1, one launch (start us, length us, event | category | flops | bytes accessed | tf_op | source)
XLA Modules:
  0.0 103.5 jit_solution(13392510680402377950)
XLA Ops:
  0.6 0.0 copy-start.5
  1.3 0.0 copy-done.5
  1.3 0.1 broadcast_in_dim.3
  1.4 0.7 broadcast_in_dim_reshape.3.skip_ref
  2.0 95.9 %layer.1 = (f32[128,512]{1,0:T(8,128)}, f32[128,512]{1,0:T(8,128)}, f32[128,128]{1,0:T(8,128)}, f32[128,128]{1,0:T(8,128)}, f32[2,4,512]{2,1,0:T(4,128)}, /*index=5*/f32[2,4,512]{2,1,0:T(4,128)}) custom-call(s32[1]{0:T(128)S(6)} %copy.21.lang_ref, f32[128,512]{1,0:T(8,128)} %x_ref.1, f32[8,128]{1,0:T(8,128)} %ld_ref.1, f32[128,128]{1,0:T(8,128)} %b_ref.1, ...), custom_call_target="tpu_custom_call" | custom-call | tf_op jit(solution)/shard_map/layer/pallas_call | solution.py:361
  98.0 0.0 copy-start
  98.0 1.7 %copy.22 = f32[128,512]{1,0:T(8,128)} copy(f32[128,512]{1,0:T(8,128)} %get-tuple-element.24) | data formatting | bytes 524288
  99.7 0.0 copy-done
  99.7 0.0 copy-start.2
  99.7 0.7 copy.23
  100.4 0.2 copy-done.2
  100.6 0.0 copy-start.1
  100.6 0.6 copy.24
  101.2 0.2 copy-done.1
  101.4 0.0 copy-start.4
  101.4 0.6 copy.25
  102.1 0.1 copy-done.4
  102.1 0.0 copy-start.3
  102.1 0.6 copy.26
  102.8 0.1 copy-done.3
  102.9 0.6 copy.27
Async XLA Ops:
  0.6 0.7 copy-start.5
  98.0 1.7 %copy-start = (f32[128,512]{1,0:T(8,128)S(1)}, f32[128,512]{1,0:T(8,128)}, u32[]{:S(2)}) copy-start(f32[128,512]{1,0:T(8,128)} %get-tuple-element.25) | copy-start | bytes 786436
  99.7 0.9 copy-start.2
  100.6 0.9 copy-start.1
  101.4 0.7 copy-start.4
  102.1 0.7 copy-start.3

commit v4 on v3

--- a/solution.py
+++ b/solution.py
@@ -11,9 +11,11 @@
 NY = 8
 NZ = 8
 NMOD = 8
+HALF = 32
 f32 = jnp.float32
 MESH = pl.DeviceIdType.MESH
 VM = pl.BlockSpec(memory_space=pltpu.VMEM)
+SM = pl.BlockSpec(memory_space=pltpu.SMEM)
 DMA = pltpu.SemaphoreType.DMA
 
 
@@ -81,24 +83,24 @@
     return total
 
 
-def row_prefix(reverse, y, gat, gaux, pre, pdec):
-    state = jnp.zeros((P_SIZE, 128), f32)
+def row_prefix(reverse, y, rows, gat, gaux, pre, pdec):
+    state = jnp.zeros((HALF, 128), f32)
     dec = jnp.ones((1, 128), f32)
     for s in range(NY - 1, -1, -1) if reverse else range(NY):
         slot = (y - s + NY) % NY
-        pre[s] = state
+        pre[s, rows] = state
         pdec[s] = jnp.broadcast_to(dec, (8, 128))
         dd = gaux[slot][0:1]
-        state = dd * state + gat[slot]
+        state = dd * state + gat[slot, rows]
         dec = dd * dec
     return state, dec
 
 
-def row_carry(reverse, z, state_of, dec_of):
-    carry = jnp.zeros((P_SIZE, 128), f32)
+def row_carry(reverse, z, rows, zg, auxz):
+    carry = jnp.zeros((HALF, 128), f32)
     for s in range(NZ - 1, -1, -1) if reverse else range(NZ):
         slot = (z - s + NZ) % NZ
-        nxt = dec_of(slot) * carry + state_of(slot)
+        nxt = auxz[slot][0:1] * carry + zg[slot, rows]
         use = (z < s) if reverse else (z > s)
         carry = jnp.where(use, nxt, carry)
     return carry
@@ -122,14 +124,14 @@
 def layer_kernel(
     lang_ref, x_ref, ld_ref, b_ref, c_ref, skip_ref, down_ref, up_ref, cot_ref,
     out_ref, ig_ref, bsum_ref, csum_ref, downg_ref, upg_ref,
-    st, aux, gat, gaux, pre, pdec, tot, zg, ret, retin,
+    st, aux, gat, gaux, pre, pdec, tot, tile, zg, ret, retin,
     back, bbuf, bacc, bag, part, rbuf, racc, rag,
     st2, gat2, tot2, zg2, ret2, retin2,
     g, abuf, apart, azbuf, zbuf, zpart, zybuf, auxz,
     cpart, cbuf, cacc, cag, bpart, xbuf, xacc, xag,
     mix, dmask, hid, headf, tailf, ghs, wg,
-    s1, r1, s2, r2, s3, r3, s4, r4, s5, r5, s6, r6, s7, r7, s8, r8,
-    t1, q1, t3, q3, t4, q4, t5, q5, t6, q6, t7, q7, t8, q8,
+    s1, r1, s3, r3, s4, r4, t1, q1, t3, q3, t4, q4,
+    s2, r2, s9, r9, s5, r5, s6, r6, s7, r7, s8, r8, t5, q5, t6, q6, t7, q7, t8, q8,
     sa, ra, sb, rb, sc, rc, sd, rd, se, re, sf, rf,
 ):
     z, y, m = ctx_place()
@@ -142,6 +144,16 @@
     sq = (128, 128)
     lower = iota(sq, 0) >= iota(sq, 1)
     left = iota(sq, 1) < P_SIZE
+    halves = [pl.ds(HALF * k, HALF) for k in range(2)]
+
+    def send_rows(pick, dst, ss, rs, dev, k):
+        out = []
+        for d in range(1, 8):
+            cp = rcopy(pick(d, halves[k]), dst.at[d, halves[k]], ss.at[k, d], rs.at[k, d], dev(d))
+            cp.start()
+            out.append(cp)
+        return out
+
     pairs = [slice(128 * p, 128 * p + 128) for p in range(4)]
 
     def spread(v, p):
@@ -175,7 +187,9 @@
     pl.semaphore_wait(pltpu.get_barrier_semaphore(), 21)
 
     c2 = send_all(lambda d: aux.at[(y + d) % NY], gaux, s2, r2, ydev)
-    c1 = send_all(lambda d: st.at[(y + d) % NY], gat, s1, r1, ydev)
+    c1 = [
+        send_rows(lambda d, r: st.at[(y + d) % NY, r], gat, s1, r1, ydev, k) for k in range(2)
+    ]
     gat[0] = st[y]
     gaux[0] = aux[y]
     back[...] = dot3(cot_ref[...], up_ref[lang], 1, 1).reshape(NMOD, 16, R)
@@ -192,38 +206,43 @@
             dmask[h] = dm
             mix[h] = dm * scores
             got.append(dot3(mix[h], xp, 1, 0))
-        hid[:, pairs[p]] = jnp.where(left, got[0], got[1]) + skip_ref[:, pairs[p]] * xp
-    arrive(c2 + c1)
-    state, dec = row_prefix(False, y, gat, gaux, pre, pdec)
-    tot[0:P_SIZE] = state
-    tot[P_SIZE:] = jnp.where(top_row, jnp.broadcast_to(dec, (8, 128)), lang_tile)
-    c3 = send_all(lambda d: tot, zg, s3, r3, zdev)
+        hid[:, pairs[p]] = jnp.where(left, got[0], got[1]) + jnp.where(left, skip_ref[2 * p], skip_ref[2 * p + 1]) * xp
+    arrive(c2)
+    c3, c4, c9 = [], [], []
+    for k in range(2):
+        arrive(c1[k])
+        state, dec = row_prefix(False, y, halves[k], gat, gaux, pre, pdec)
+        if k == 0:
+            tile[...] = jnp.where(top_row, jnp.broadcast_to(dec, (8, 128)), lang_tile)
+            c9 = send_all(lambda d: tile, auxz, s9, r9, zdev)
+        tot[halves[k]] = state
+        c3.append(send_rows(lambda d, r: tot.at[r], zg, s3, r3, zdev, k))
     bacc[...] = add_up(back[m], c5, bbuf)
     c6 = send_all(lambda d: bacc, bag, s6, r6, mdev)
     zg[0] = tot[...]
     bag[0] = bacc[...]
-    arrive(c3)
-    carry = row_carry(
-        False, z, lambda i: zg[i, 0:P_SIZE], lambda i: zg[i, P_SIZE : P_SIZE + 8][0:1]
-    )
-
-    def send_back(pre, carry, ret, retin, ss, rs):
+    auxz[0] = tile[...]
+    arrive(c9)
+
+    def send_back(k, carry, ret, retin, ss, rs):
+        r = halves[k]
         out = []
         for d in range(1, NY):
             s = (y + d) % NY
-            ret[d] = pre[s] + pdec[s][0:1] * carry
-            cp = rcopy(ret.at[d], retin.at[d], ss.at[d], rs.at[d], ydev(d))
+            ret[d, r] = pre[s, r] + pdec[s][0:1] * carry
+            cp = rcopy(ret.at[d, r], retin.at[d, r], ss.at[k, d], rs.at[k, d], ydev(d))
             cp.start()
             out.append(cp)
-        retin[0] = pre[y] + pdec[y][0:1] * carry
+        retin[0, r] = pre[y, r] + pdec[y][0:1] * carry
         return out
 
     def in_order(buf, place):
         return jnp.concatenate([buf[(place - h + 8) % 8] for h in range(8)], axis=0)
 
-    c4 = send_back(pre, carry, ret, retin, s4, r4)
-    for d in range(NZ):
-        auxz[d] = zg[d, P_SIZE:]
+    for k in range(2):
+        arrive(c3[k])
+        carry = row_carry(False, z, halves[k], zg, auxz)
+        c4 += send_back(k, carry, ret, retin, s4, r4)
     arrive(c6)
     back_act = in_order(bag, m)
     arrive(c4)
@@ -244,7 +263,9 @@
     ghs[...] = gh
     head_gh = headf[...] * gh
     st2[...] = dot3(head_gh, c, 0, 0).reshape(8, P_SIZE, 128)
-    e1 = send_all(lambda d: st2.at[(y + d) % NY], gat2, t1, q1, ydev)
+    e1 = [
+        send_rows(lambda d, r: st2.at[(y + d) % NY, r], gat2, t1, q1, ydev, k) for k in range(2)
+    ]
     gat2[0] = st2[y]
 
     col = iota((R, 2 * R), 1)
@@ -285,10 +306,11 @@
         weighted = weighted + dmask[2 * p + 1] * dot3(jnp.where(left, 0.0, gp), xp, 1, 1)
     cpart[...] = (dot3(weighted, b, 1, 0) + dot3(head_gh, state_in, 1, 0)).reshape(8, 16, 128)
     e5 = send_all(lambda d: cpart.at[(m + d) % NMOD], cbuf, t5, q5, mdev)
-    arrive(e1)
-    state, _ = row_prefix(True, y, gat2, gaux, pre, pdec)
-    tot2[...] = state
-    e3 = send_all(lambda d: tot2, zg2, t3, q3, zdev)
+    e3, e4 = [], []
+    for k in range(2):
+        arrive(e1[k])
+        tot2[halves[k]], _ = row_prefix(True, y, halves[k], gat2, gaux, pre, pdec)
+        e3.append(send_rows(lambda d, r: tot2.at[r], zg2, t3, q3, zdev, k))
     cb1 = send_half(True, 1, sd, rd)
     ca0 = send_half(False, 0, sa, ra)
     zg2[0] = tot2[...]
@@ -296,9 +318,10 @@
     e6 = send_all(lambda d: cacc, cag, t6, q6, mdev)
     out_ref[...] = hid[...] + dot3(active, up_ref[lang], 1, 0)
     b_part = dot3(weighted, c, 0, 0)
-    arrive(e3)
-    carry = row_carry(True, z, lambda i: zg2[i], lambda i: auxz[i][0:1])
-    e4 = send_back(pre, carry, ret2, retin2, t4, q4)
+    for k in range(2):
+        arrive(e3[k])
+        carry = row_carry(True, z, halves[k], zg2, auxz)
+        e4 += send_back(k, carry, ret2, retin2, t4, q4)
     ca1 = send_half(False, 1, sb, rb)
     zbuf[0] = g[1, z]
     for t in range(NZ):
@@ -308,7 +331,7 @@
         gp = ghs[:, pairs[p]]
         ig_ref[:, pairs[p]] = (
             jnp.where(left, dot3(mix[2 * p], gp, 0, 0), dot3(mix[2 * p + 1], gp, 0, 0))
-            + skip_ref[:, pairs[p]] * gp
+            + jnp.where(left, skip_ref[2 * p], skip_ref[2 * p + 1]) * gp
         )
     arrive(e6)
     csum_ref[...] = in_order(cag, m)
@@ -332,7 +355,9 @@
     wg[:, :, :256] = add_up(apart[z], cf, azbuf)
     downg_ref[...] = wg[:, 0:4, :]
     upg_ref[...] = wg[:, 4:8, :]
-    for cp in c1 + c2 + c3 + c4 + c5 + c6 + c7 + c8 + e1 + e3 + e4 + e5 + e6 + e7 + e8:
+    for cp in c1[0] + c1[1] + c2 + c3[0] + c3[1] + c4 + c5 + c6 + c7 + c8 + c9:
+        cp.wait_send()
+    for cp in e1[0] + e1[1] + e3[0] + e3[1] + e4 + e5 + e6 + e7 + e8:
         cp.wait_send()
     for cp in ca0 + ca1 + cb0 + cb1 + ce + cf:
         cp.wait_send()
@@ -351,7 +376,7 @@
     act, proj = (8, 16, R), (8, 16, 128)
     big, mid = (8, 8, 8, 256), (8, LANG, 8, 256)
     shapes = [
-        st, tile, st, tile, st, tile, (P_SIZE + 8, 128), (8, P_SIZE + 8, 128), st, st,
+        st, tile, st, tile, st, tile, st[1:], tile[1:], st, st, st,
         act, act, act[1:], act, act, act, act[1:], act,
         st, st, st[1:], st, st, st,
         (2,) + big, big, mid, mid, big, mid, mid, tile,
@@ -365,9 +390,9 @@
             out_of(*wide), out_of(*wide), out_of(128, 128), out_of(128, 128),
             out_of(LANG, 4, 512), out_of(LANG, 4, 512),
         ),
-        in_specs=[pl.BlockSpec(memory_space=pltpu.SMEM)] + [VM] * 8,
+        in_specs=[SM] + [VM] * 4 + [SM] + [VM] * 3,
         out_specs=(VM,) * 6,
-        scratch_shapes=[vmem(*s) for s in shapes] + [DMA((8,))] * 42,
+        scratch_shapes=[vmem(*s) for s in shapes] + [DMA((2, 8))] * 12 + [DMA((8,))] * 32,
         compiler_params=pltpu.CompilerParams(collective_id=1, has_side_effects=True),
     )(*args)
 
@@ -375,9 +400,8 @@
 def shards(
     seq_input, log_decay, b_proj, c_proj, skip_gain, down_weight, up_weight, block_lang, cotangent
 ):
-    skip = jnp.repeat(skip_gain, P_SIZE)[None, :]
     layer_out, input_grad, b_grad, c_grad, down_t, up_grad = layer_call(
-        block_lang, seq_input, log_decay, b_proj, c_proj, skip, down_weight, up_weight, cotangent
+        block_lang, seq_input, log_decay, b_proj, c_proj, skip_gain, down_weight, up_weight, cotangent
     )
     return layer_out, input_grad, b_grad, c_grad, down_t.transpose(0, 2, 1), up_grad
 

time: 104 us -> 97.7 us (0.939)
  Pallas kernels: 95.9 us -> 90.5 us
    pallas_call x1, Pallas kernels: 95.9 us -> 90.5 us  [layer_call(): pl.pallas_call(layer_kernel, name='layer', out_shape=(out_of(*wide), out_...]
    unnamed x18 -> x16, local copies, waits for them, and re-layouts: 5.49 us -> 5.49 us
where the time goes in v4:
time: 97.7 us; the launch traced here: 97.3 us
  Pallas kernels  90.5 us (93%)
  local copies, waits for them, and re-layouts  5.49 us (6%)
  between operations  1.3 us (1%)
    pallas_call x1, Pallas kernels, layer_call(): pl.pallas_call(layer_kernel, name='layer', out_shape=(out_of(*wide), out_...  90.5 us
    unnamed x16, local copies, waits for them, and re-layouts  5.49 us

profile of v4, /device:TPU:1, one launch (start us, length us, event | category | flops | bytes accessed | tf_op | source)
XLA Modules:
  0.0 97.3 jit_solution(5318575474282961060)
XLA Ops:
  1.3 90.5 %layer.1 = (f32[128,512]{1,0:T(8,128)}, f32[128,512]{1,0:T(8,128)}, f32[128,128]{1,0:T(8,128)}, f32[128,128]{1,0:T(8,128)}, f32[2,4,512]{2,1,0:T(4,128)}, /*index=5*/f32[2,4,512]{2,1,0:T(4,128)}) custom-call(s32[1]{0:T(128)S(6)} %copy.21.lang_ref, f32[128,512]{1,0:T(8,128)} %x_ref.1, f32[8,128]{1,0:T(8,128)} %ld_ref.1, f32[128,128]{1,0:T(8,128)} %b_ref.1, ...), custom_call_target="tpu_custom_call" | custom-call | tf_op jit(solution)/shard_map/layer/pallas_call | solution.py:386
  91.8 0.0 copy-start
  91.8 1.7 %copy.22 = f32[128,512]{1,0:T(8,128)} copy(f32[128,512]{1,0:T(8,128)} %get-tuple-element.24) | data formatting | bytes 524288
  93.5 0.0 copy-done
  93.5 0.0 copy-start.2
  93.5 0.7 copy.23
  94.2 0.2 copy-done.2
  94.4 0.0 copy-start.1
  94.4 0.6 copy.24
  95.0 0.2 copy-done.1
  95.3 0.0 copy-start.4
  95.3 0.6 copy.25
  95.9 0.1 copy-done.4
  96.0 0.0 copy-start.3
  96.0 0.6 copy.26
  96.6 0.1 copy-done.3
  96.7 0.6 copy.27
Async XLA Ops:
  91.8 1.7 %copy-start = (f32[128,512]{1,0:T(8,128)S(1)}, f32[128,512]{1,0:T(8,128)}, u32[]{:S(2)}) copy-start(f32[128,512]{1,0:T(8,128)} %get-tuple-element.25) | copy-start | bytes 786436
  93.5 0.9 copy-start.2
  94.4 0.9 copy-start.1
  95.3 0.7 copy-start.4
  96.0 0.7 copy-start.3
